TPU v7x, 256 devices: a whole 4x4x8 slice. The times are simulated.
256 devices in a mesh: seq: 64 (over x, z, core), batch: 4 (over y).
Axes of the slice: x: 4, y: 4, z: 8, core: 2. Of those that a mesh axis runs over, the one named last changes fastest.
Arguments:
- inputs: float32 [8, 16384, 256], P('batch', 'seq'), may hold values from -6 to 6
- guess_path: float32 [8, 16384, 128], P('batch', 'seq'), may hold values from -3 to 3
- recur_weight: float32 [128, 128], replicated, may hold values from -0.09 to 0.09
- damping: float32 [128], replicated, may hold values from 0.00024414062 to 2.5
- in_weight: float32 [256, 128], replicated, may hold values from -0.375 to 0.375
- bias_term: float32 [128], replicated, may hold values from -3 to 3
- targets: float32 [8, 128, 128], P('batch', 'seq'), may hold values from -6 to 6
- target_steps: int32 [8, 128], P('batch', 'seq'), may hold values from 0 to 127
Outputs:
- trajectory: float32 [8, 16384, 128], P('batch', 'seq')
- grad_recur: float32 [128, 128], replicated
- grad_in: float32 [256, 128], replicated
All inputs are finite; a program needn't handle non-finite values.
Results may differ from a plain program's by a relative error of at most 0.0003.
Values sent between devices are 32-bit elements; how exact they have to be, the bound alone decides.
A program may use at most 64 MiB of HBM per device.

v0:
```python
import jax
import jax.numpy as jnp
from jax import lax
from jax.sharding import Mesh
from jax.sharding import PartitionSpec as P

BLK = 16
TBLK = 128
SEQ = ("seq_0", "seq_1", "seq_2")


euler_step = 0.02


def shifted(block, axis, distance):
    devices = range(lax.axis_size(axis))
    route = [(i - distance, i) for i in devices if i - distance in devices]
    return lax.ppermute(block, axis, route)


def neutral_like(shard, identity):
    return jax.tree.map(
        lambda part, zero: jnp.zeros_like(part) + jnp.asarray(zero, part.dtype), shard, identity
    )


def prefix_by_axis(shard, axes, combine, identity, reverse):
    before = start = neutral_like(shard, identity)
    subtotal = shard
    for axis in reversed(axes):
        length, place = (lax.axis_size(axis), lax.axis_index(axis))
        pieces = jax.tree.map(lambda part: lax.all_gather(part, axis), subtotal)
        inside, subtotal = (start, start)
        for k in reversed(range(length)) if reverse else range(length):
            passed = k > place if reverse else k < place
            subtotal = combine(subtotal, jax.tree.map(lambda part: part[k], pieces))
            inside = jax.tree.map(lambda new, old: jnp.where(passed, new, old), subtotal, inside)
        before = combine(inside, before)
    return before


def split_up(shard, dim, length):
    before, after = (shard.shape[:dim], shard.shape[dim + 1 :])
    return jnp.moveaxis(shard.reshape(*before, length, -1, *after), dim, 0)


def sent_and_summed(shard, axis, dim):
    tiles = split_up(shard, dim, lax.axis_size(axis))
    arrived = lax.all_to_all(tiles, axis, split_axis=0, concat_axis=0, tiled=True)
    return arrived.sum(axis=0)


def sum_by_axis(shard, axes, dim):
    far, near = axes
    own = sent_and_summed(split_up(shard, dim, lax.axis_size(far)), near, dim + 1)
    return jnp.sum(lax.all_to_all(own, far, 0, 0, tiled=True), axis=0)


def rows_for(lines, length):
    spare = -len(lines) % length
    return jnp.pad(lines, [(0, spare)] + [(0, 0)] * (lines.ndim - 1))


def copy_for_each(shard, axis):
    length = lax.axis_size(axis)
    return lax.all_to_all(
        jnp.broadcast_to(shard[None], (length, *shard.shape)), axis, 0, 0, tiled=True
    )


def in_order(tiles, dim):
    tiles = jnp.moveaxis(tiles, 0, dim)
    dims = tiles.shape
    return tiles.reshape(*dims[:dim], dims[dim] * dims[dim + 1], *dims[dim + 2 :])


def gather_axes(shard, axes, dim):
    far, near = axes
    initial = copy_for_each(shard, far)
    tiles = jnp.swapaxes(copy_for_each(initial, near), 0, 1)
    return in_order(tiles.reshape(-1, *shard.shape), dim)


def sum_by_parts(shard, axes):
    lines = shard.reshape(-1)
    own = sum_by_axis(rows_for(lines, lax.axis_size(axes[0]) * lax.axis_size(axes[1])), axes, 0)
    whole = gather_axes(own, axes, 0)
    return whole[: len(lines)].reshape(shard.shape)


def join_maps(earlier, later):
    highest = lax.Precision.HIGHEST
    matrix = jnp.einsum("isk,ksj->isj", later[0], earlier[0], precision=highest)
    vector = jnp.einsum("isj,sj->si", later[0], earlier[1], precision=highest) + later[1]
    return (matrix, vector)


def apply_map(carry, inputs_now):
    block_map, block_off = inputs_now
    result = jnp.einsum("isj,sj->si", block_map, carry, precision=lax.Precision.HIGHEST) + block_off
    return (result, carry)


def on_device(
    inputs, guess_path, recur_weight, damping, in_weight, bias_term, targets, target_steps
):
    highest = lax.Precision.HIGHEST
    seq_count, step_count, hidden = guess_path.shape
    block_count = step_count // BLK
    lane_count = seq_count * block_count
    skew = recur_weight - recur_weight.T
    skew_t = skew.T
    edge = shifted(guess_path[:, step_count - 1, :], SEQ, 1)
    prev = jnp.concatenate([edge[:, None, :], guess_path[:, :-1, :]], axis=1)
    drive = jnp.dot(
        inputs.reshape(seq_count * step_count, -1), in_weight, precision=highest
    ).reshape(seq_count, step_count, hidden)
    preact = jnp.dot(prev.reshape(-1, hidden), skew_t, precision=highest).reshape(
        seq_count, step_count, hidden
    )
    preact = preact - damping * prev + drive + bias_term
    activation = jnp.tanh(preact)
    gain = euler_step * (1.0 - activation * activation)
    resid = prev + euler_step * activation - guess_path

    def by_step(values):
        return (
            values.reshape(seq_count, block_count, BLK, hidden)
            .transpose(2, 0, 1, 3)
            .reshape(BLK, lane_count, hidden)
        )

    def from_step(values):
        return (
            values.reshape(BLK, seq_count, block_count, hidden)
            .transpose(1, 2, 0, 3)
            .reshape(seq_count, step_count, hidden)
        )

    gain_steps = by_step(gain)
    resid_steps = by_step(resid)

    def advance(state, gain_now, resid_now):
        moved = jnp.dot(state, skew_t, precision=highest) - damping * state
        return state + gain_now * moved + resid_now

    def compose(carry, inputs_now):
        maps, offsets = carry
        gain_now, resid_now = inputs_now
        turned = jnp.dot(
            skew, maps.reshape(hidden, lane_count * hidden), precision=highest
        ).reshape(hidden, lane_count, hidden)
        turned = turned - damping[:, None, None] * maps
        maps = maps + gain_now.T[:, :, None] * turned
        offsets = advance(offsets, gain_now, resid_now)
        return ((maps, offsets), None)

    unit_map = jnp.eye(hidden, dtype=jnp.float32)
    lane_zero = jnp.zeros((lane_count, hidden), jnp.float32)
    start_maps = jnp.broadcast_to(unit_map[:, None, :], (hidden, lane_count, hidden))
    (block_maps, block_offs), _ = lax.scan(
        compose, (start_maps, lane_zero), (gain_steps, resid_steps)
    )
    blocks = block_maps.reshape(hidden, seq_count, block_count, hidden).transpose(2, 0, 1, 3)
    offsets = block_offs.reshape(seq_count, block_count, hidden).transpose(1, 0, 2)

    def chain(carry, inputs_now):
        total, offset = carry
        block_map, block_off = inputs_now
        total = jnp.einsum("isk,ksj->isj", block_map, total, precision=highest)
        offset = jnp.einsum("isj,sj->si", block_map, offset, precision=highest) + block_off
        return ((total, offset), None)

    seq_zero = jnp.zeros((seq_count, hidden), jnp.float32)
    unit_stack = jnp.broadcast_to(unit_map[:, None, :], (hidden, seq_count, hidden))
    (dev_map, dev_off), _ = lax.scan(chain, (unit_stack, seq_zero), (blocks, offsets))
    _, delta_in = prefix_by_axis((dev_map, dev_off), SEQ, join_maps, (unit_stack, seq_zero), False)
    _, starts = lax.scan(apply_map, delta_in, (blocks, offsets))
    starts = starts.transpose(1, 0, 2).reshape(lane_count, hidden)

    def forward(state, inputs_now):
        state = advance(state, inputs_now[0], inputs_now[1])
        return (state, state)

    _, deltas = lax.scan(forward, starts, (gain_steps, resid_steps))
    trajectory = guess_path + from_step(deltas)
    total_seqs = seq_count * lax.axis_size("batch")
    target_blocks = step_count // TBLK
    target_hit = (jnp.arange(TBLK)[None, None, :] == target_steps[:, :, None]).astype(jnp.float32)
    miss = trajectory.reshape(seq_count, target_blocks, TBLK, hidden) - targets[:, :, None, :]
    source = (target_hit[..., None] * miss / total_seqs).reshape(seq_count, step_count, hidden)
    source_steps = by_step(source)

    def retreat(carry, inputs_now):
        gain_now, source_now = inputs_now
        adjoint = source_now + carry
        scaled = gain_now * adjoint
        carry = adjoint + jnp.dot(scaled, skew, precision=highest) - damping * scaled
        return (carry, adjoint)

    outflow, _ = lax.scan(retreat, lane_zero, (gain_steps, source_steps), reverse=True)
    outflow = outflow.reshape(seq_count, block_count, hidden).transpose(1, 0, 2)
    flipped = blocks.transpose(0, 3, 2, 1)
    adjoint_off, _ = lax.scan(apply_map, seq_zero, (flipped, outflow), reverse=True)
    dev_flipped = dev_map.transpose(2, 1, 0)
    _, adjoint_in = prefix_by_axis(
        (dev_flipped, adjoint_off), SEQ, join_maps, (unit_stack, seq_zero), True
    )
    _, block_ends = lax.scan(apply_map, adjoint_in, (flipped, outflow), reverse=True)
    block_ends = block_ends.transpose(1, 0, 2).reshape(lane_count, hidden)
    _, adjoints = lax.scan(retreat, block_ends, (gain_steps, source_steps), reverse=True)
    grad_pre = gain * from_step(adjoints)
    flat_pre = grad_pre.reshape(-1, hidden)
    recur_sum = jnp.dot(flat_pre.T, prev.reshape(-1, hidden), precision=highest)
    input_sum = jnp.dot(inputs.reshape(seq_count * step_count, -1).T, flat_pre, precision=highest)
    recur_sum, input_sum = (
        sum_by_parts(recur_sum, (("seq_0", "seq_1"), ("seq_2", "batch"))),
        sum_by_parts(input_sum, (("seq_0", "seq_1"), ("seq_2", "batch"))),
    )
    return (trajectory, recur_sum - recur_sum.T, input_sum)


def solution(mesh):
    torus = Mesh(
        mesh.devices.reshape(4, 8, 2, mesh.shape["batch"]), ("seq_0", "seq_1", "seq_2", "batch")
    )
    return jax.shard_map(
        on_device,
        mesh=torus,
        in_specs=(
            P("batch", SEQ, None),
            P("batch", SEQ, None),
            P(),
            P(),
            P(),
            P(),
            P("batch", SEQ, None),
            P("batch", SEQ),
        ),
        out_specs=(P("batch", SEQ, None), P(), P()),
        check_vma=False,
    )
```

profile of v0, /device:TPU:1, one launch (start us, length us, event | category | flops | bytes accessed | tf_op | source)
XLA Modules:
  0.0 478.1 jit_solution(15200165481536507880)
XLA Ops:
  8.0 4.9 %collective-permute-start = (f32[2,128]{1,0:T(2,128)S(1)}, f32[2,128]{1,0:T(2,128)S(1)}, u32[]{:S(2)}, u32[]{:S(2)}) collective-permute-start(f32[2,128]{1,0:T(2,128)S(1)} %bitcast.802), channel_id=1, source_target_pairs={{0,4},{4,8},{8,12},{12,16},{16,20},{20,24},{24,28},{28,32},{32,36}... | collective-permute-start | bytes 3080 | tf_op jit(solution)/shard_map/ppermute | solution.py:18
  21.5 106.7 %while.116 = (s32[]{:T(128)}, f32[128,32,128]{2,0,1:T(8,128)S(1)}, f32[32,128]{1,0:T(8,128)S(1)}, f32[16,32,128]{2,1,0:T(8,128)S(1)}, f32[128,128]{1,0:T(8,128)S...) while((s32[]{:T(128)}, f32[128,32,128]{2,0,1:T(8,128)S(1)}, ...), condition=%wide.region_1.2_spmd.clone, body=%wide.region_0.1_spmd.clone.sunk | while | flops 813723648 | bytes 10782838 | solution.py:161
  24.3 3.9 multiply_add_fusion.3
  31.0 3.9 multiply_add_fusion.3
  37.7 3.9 multiply_add_fusion.3
  44.3 3.9 multiply_add_fusion.3
  51.0 3.9 multiply_add_fusion.3
  57.7 3.9 multiply_add_fusion.3
  64.3 3.9 multiply_add_fusion.3
  71.0 3.9 multiply_add_fusion.3
  77.7 3.9 multiply_add_fusion.3
  84.3 3.9 multiply_add_fusion.3
  91.0 3.9 multiply_add_fusion.3
  97.7 3.9 multiply_add_fusion.3
  104.4 3.9 multiply_add_fusion.3
  111.0 3.9 multiply_add_fusion.3
  117.7 3.9 multiply_add_fusion.3
  124.4 3.9 multiply_add_fusion.3
  128.3 10.5 %while.117 = (s32[]{:T(128)}, f32[128,2,128]{2,0,1:T(8,128)S(1)}, f32[2,128]{1,0:T(2,128)S(1)}, f32[16,128,2,128]{3,1,0,2:T(8,128)S(1)}, f32[16,2,128]{2,1,0:T(2,128)S(1)}, /*index=5*/s32[]{:T(128)}, s32[]{:T(128)}) while((s32[]{:T(128)}, f32[128,2,128]{2,0,1:T(8,128)S(1)}, f32[2,128]{1,0:T(2,128)S(1)}, ...), condition=%wide.region_3.4_spmd.clone, body=%wide.region_2.3_spmd.clone.sunk | while | flops 50725376 | bytes 793699 | solution.py:176
  150.8 14.8 %all-gather.13 = f32[8,2,128]{2,1,0:T(2,128)} all-gather(f32[1,2,128]{2,1,0:T(2,128)S(1)} %get-tuple-element.911), channel_id=6, replica_groups=mesh['seq_0'=4,'seq_1'=8,'seq_2'=2,'batch'=4] {'seq_1'}, dimensions={0}, use_global_device_ids=true | all-gather | bytes 9216 | tf_op jit(solution)/shard_map/all_gather | solution.py:32
  165.5 5.8 %all-gather.6 = f32[256,2,128]{2,0,1:T(8,128)S(1)} all-gather(f32[128,2,128]{2,0,1:T(8,128)} %bitcast.713), channel_id=8, replica_groups=mesh['seq_0'=4,'seq_1'=8,'seq_2'=2,'batch'=4] {'seq_2'}, dimensions={0}, use_global_device_ids=true | all-gather | bytes 393216 | tf_op jit(solution)/shard_map/all_gather | solution.py:32
  175.9 8.8 %all-gather.21.cloned.1.call-done = f32[1024,2,128]{0,2,1:T(8,128)} async-done(((f32[128,2,128]{0,2,1:T(8,128)}), f32[1024,2,128]{0,2,1:T(8,128)}) %all-gather.21.cloned.1.call-update) | async-done | bytes 1048592 | tf_op jit(solution)/shard_map/all_gather | solution.py:32
  202.4 11.2 %all-gather.2 = f32[512,2,128]{0,2,1:T(8,128)S(1)} all-gather(f32[128,2,128]{0,2,1:T(8,128)S(1)} %convolution_bitcast_fusion.16), channel_id=4, replica_groups=mesh['seq_0'=4,'seq_1'=8,'seq_2'=2,'batch'=4] {'seq_0'}, dimensions={0}, use_global_device_ids=true | all-gather | bytes 655360 | tf_op jit(solution)/shard_map/all_gather | solution.py:32
  215.0 7.6 %all-gather.14 = f32[4,2,128]{2,1,0:T(2,128)S(1)} all-gather(f32[1,2,128]{2,1,0:T(2,128)S(1)} %get-tuple-element.907), channel_id=7, replica_groups=mesh['seq_0'=4,'seq_1'=8,'seq_2'=2,'batch'=4] {'seq_0'}, dimensions={0}, use_global_device_ids=true | all-gather | bytes 5120 | tf_op jit(solution)/shard_map/all_gather | solution.py:32
  223.9 18.2 %while.112 = (s32[]{:T(128)}, f32[2,128]{1,0:T(2,128)S(1)}, f32[16,2,128]{2,1,0:T(2,128)S(1)}, f32[16,128,2,128]{3,1,0,2:T(8,128)S(1)}, f32[16,2,128]{2,1,0:T(2,128)}, /*index=5*/s32[]{:T(128)}) while((s32[]{:T(128)}, f32[2,128]{1,0:T(2,128)S(1)}, f32[16,2,128]{2,1,0:T(2,128)S(1)}, f32[16,128,2,128]{3,1,0,2:T(8,128)S(1)}, ...), condition=%wide.region_5.6_spmd, body=%wide.region_4.5_spmd.sunk | while | flops 393474 | bytes 662609 | solution.py:178
  242.1 14.9 %while.113 = (s32[]{:T(128)}, f32[32,128]{1,0:T(8,128)S(1)}, f32[16,32,128]{2,1,0:T(8,128)S(1)}, f32[16,32,128]{2,1,0:T(8,128)S(1)}, f32[128,128]{1,0:T(8,128)S(...) while((s32[]{:T(128)}, f32[32,128]{1,0:T(8,128)S(1)}, f32[16,32,128]{2,1,0:T(8,128)S(1)}, ...), condition=%wide.region_7.8_spmd, body=%wide.region_6.7_spmd.sunk | while | flops 6311938 | bytes 197209 | solution.py:185
  261.0 20.2 %while.119 = (s32[]{:T(128)}, f32[2,128]{1,0:T(2,128)S(1)}, f32[16,128,2,128]{3,2,1,0:T(2,128)}, f32[16,2,128]{2,1,0:T(2,128)S(1)}, s32[]{:T(128)}, /*index=5*/s32[]{:T(128)}, s32[]{:T(128)}) while((s32[]{:T(128)}, f32[2,128]{1,0:T(2,128)S(1)}, f32[16,128,2,128]{3,2,1,0:T(2,128)}, f32[16,2,128]{2,1,0:T(2,128)S(1)}, s32[]{:T(128)}, ...), condition=%wide.region_11.12_spmd.clone, body=%wide.region_10.11_spmd.clone.sunk | while | flops 393732 | bytes 400491 | solution.py:204
  281.2 10.5 %all-gather.15 = f32[2,2,128]{2,1,0:T(2,128)S(1)} all-gather(f32[1,2,128]{2,1,0:T(2,128)S(1)} %bitcast.736), channel_id=11, replica_groups=mesh['seq_0'=4,'seq_1'=8,'seq_2'=2,'batch'=4] {'seq_2'}, dimensions={0}, use_global_device_ids=true | all-gather | bytes 3072 | tf_op jit(solution)/shard_map/all_gather | solution.py:32
  292.1 13.0 %all-gather.16 = f32[8,2,128]{2,1,0:T(2,128)} all-gather(f32[1,2,128]{2,1,0:T(2,128)S(1)} %get-tuple-element.909), channel_id=12, replica_groups=mesh['seq_0'=4,'seq_1'=8,'seq_2'=2,'batch'=4] {'seq_1'}, dimensions={0}, use_global_device_ids=true | all-gather | bytes 9216 | tf_op jit(solution)/shard_map/all_gather | solution.py:32
  323.0 11.0 %all-gather.8 = f32[512,2,128]{0,2,1:T(8,128)S(1)} all-gather(f32[128,2,128]{0,2,1:T(8,128)S(1)} %convolution_bitcast_fusion.4), channel_id=10, replica_groups=mesh['seq_0'=4,'seq_1'=8,'seq_2'=2,'batch'=4] {'seq_0'}, dimensions={0}, use_global_device_ids=true | all-gather | bytes 655360 | tf_op jit(solution)/shard_map/all_gather | solution.py:32
  335.5 5.2 %all-gather.17 = f32[4,2,128]{2,1,0:T(2,128)S(1)} all-gather(f32[1,2,128]{2,1,0:T(2,128)S(1)} %get-tuple-element.905), channel_id=13, replica_groups=mesh['seq_0'=4,'seq_1'=8,'seq_2'=2,'batch'=4] {'seq_0'}, dimensions={0}, use_global_device_ids=true | all-gather | bytes 5120 | tf_op jit(solution)/shard_map/all_gather | solution.py:32
  341.9 20.1 %while.114 = (s32[]{:T(128)}, f32[2,128]{1,0:T(2,128)S(1)}, f32[16,2,128]{2,1,0:T(2,128)S(1)}, f32[16,128,2,128]{3,2,1,0:T(2,128)}, f32[16,2,128]{2,1,0:T(2,128)S(1)}, /*index=5*/s32[]{:T(128)}, s32[]{:T(128)}) while((s32[]{:T(128)}, f32[2,128]{1,0:T(2,128)S(1)}, f32[16,2,128]{2,1,0:T(2,128)S(1)}, f32[16,128,2,128]{3,2,1,0:T(2,128)}, ...), condition=%wide.region_13.14_spmd, body=%wide.region_12.13_spmd.sunk | while | flops 393475 | bytes 400485 | solution.py:209
  362.1 3.7 while.115
  366.9 17.1 %all_to_all.50 = f32[8,1,2048]{2,1,0:T(1,128)S(1)} all-to-all(f32[8,1,2048]{2,1,0:T(1,128)S(1)} %reshape.376), channel_id=1, replica_groups=mesh['seq_0'=4,'seq_1'=8,'seq_2'=2,'batch'=4] {'seq_2','batch'}, dimensions={0} | all-to-all | bytes 131072 | tf_op jit(solution)/shard_map/all_to_all | solution.py:49
  386.0 5.4 %all-to-all-start.1 = ((f32[32,1,64]{2,1,0:T(1,128)}), f32[32,1,64]{2,1,0:T(1,128)S(1)}, u32[]{:S(2)}, u32[]{:S(2)}) async-start(f32[32,1,64]{2,1,0:T(1,128)} %bitcast.248), calls=%async_computation.1 | async-start | bytes 32768 | tf_op jit(solution)/shard_map/all_to_all | solution.py:56
  392.8 7.2 %all-to-all-done.1 = f32[32,1,64]{2,1,0:T(1,128)S(1)} async-done(((f32[32,1,64]{2,1,0:T(1,128)}), f32[32,1,64]{2,1,0:T(1,128)S(1)}, u32[]{:S(2)}, u32[]{:S(2)}) %all-to-all-start.1) | async-done | bytes 8224 | tf_op jit(solution)/shard_map/all_to_all | solution.py:56
  400.0 5.1 %all-to-all-start.4 = ((f32[8,32,128]{2,1,0:T(8,128)}), f32[8,32,128]{2,1,0:T(8,128)S(1)}, u32[]{:S(2)}, u32[]{:S(2)}) async-start(f32[8,32,128]{2,1,0:T(8,128)} %copy.195), calls=%async_computation.4 | async-start | bytes 262144 | tf_op jit(solution)/shard_map/all_to_all | solution.py:49
  405.2 5.1 %all-to-all-done.4 = f32[8,32,128]{2,1,0:T(8,128)S(1)} async-done(((f32[8,32,128]{2,1,0:T(8,128)}), f32[8,32,128]{2,1,0:T(8,128)S(1)}, u32[]{:S(2)}, u32[]{:S(2)}) %all-to-all-start.4) | async-done | bytes 131104 | tf_op jit(solution)/shard_map/all_to_all | solution.py:49
  411.0 3.8 all-to-all-start.2
  415.4 8.0 %all-to-all-done.2 = f32[32,1,64]{2,1,0:T(1,128)S(1)} async-done(((f32[32,1,64]{2,1,0:T(1,128)}), f32[32,1,64]{2,1,0:T(1,128)S(1)}, u32[]{:S(2)}, u32[]{:S(2)}) %all-to-all-start.2) | async-done | bytes 8224 | tf_op jit(solution)/shard_map/all_to_all | solution.py:66
  423.4 3.8 all-to-all-start.5
  428.0 7.8 %all-to-all-done.5 = f32[32,1,128]{2,1,0:T(1,128)S(1)} async-done(((f32[32,1,128]{2,1,0:T(1,128)}), f32[32,1,128]{2,1,0:T(1,128)S(1)}, u32[]{:S(2)}, u32[]{:S(2)}) %all-to-all-start.5) | async-done | bytes 16416 | tf_op jit(solution)/shard_map/all_to_all | solution.py:56
  435.8 6.0 %all-to-all-start.3 = ((f32[8,1,2048]{2,1,0:T(1,128)}), f32[8,1,2048]{2,1,0:T(1,128)S(1)}, u32[]{:S(2)}, u32[]{:S(2)}) async-start(f32[8,1,2048]{2,1,0:T(1,128)} %reshape.378), calls=%async_computation.3 | async-start | bytes 131072 | tf_op jit(solution)/shard_map/all_to_all | solution.py:66
  441.8 4.9 %all-to-all-done.3 = f32[8,1,2048]{2,1,0:T(1,128)S(1)} async-done(((f32[8,1,2048]{2,1,0:T(1,128)}), f32[8,1,2048]{2,1,0:T(1,128)S(1)}, u32[]{:S(2)}, u32[]{:S(2)}) %all-to-all-start.3) | async-done | bytes 65568 | tf_op jit(solution)/shard_map/all_to_all | solution.py:66
  447.4 3.8 all-to-all-start.6
  452.3 7.5 %all-to-all-done.6 = f32[32,1,128]{2,1,0:T(1,128)S(1)} async-done(((f32[32,1,128]{2,1,0:T(1,128)}), f32[32,1,128]{2,1,0:T(1,128)S(1)}, u32[]{:S(2)}, u32[]{:S(2)}) %all-to-all-start.6) | async-done | bytes 16416 | tf_op jit(solution)/shard_map/all_to_all | solution.py:66
  460.5 4.8 %all-to-all-start.7 = ((f32[8,32,128]{2,1,0:T(8,128)}), f32[8,32,128]{2,1,0:T(8,128)S(1)}, u32[]{:S(2)}, u32[]{:S(2)}) async-start(f32[8,32,128]{2,1,0:T(8,128)} %broadcast_in_dim.121), calls=%async_computation.7 | async-start | bytes 262144 | tf_op jit(solution)/shard_map/all_to_all | solution.py:66
  465.9 4.6 all-to-all-done.7
  (660 shorter events, 213.1 us)
Async XLA Ops:
  7.2 9.2 %copy-start = (f32[2,256,256]{2,1,0:T(8,128)S(1)}, f32[2,256,256]{2,1,0:T(8,128)}, u32[]{:S(2)}) copy-start(f32[2,256,256]{2,1,0:T(8,128)} %param.24) | copy-start | bytes 1572868
  7.2 177.6 %all-gather.21.cloned.1.call-start = ((), (), s32[]{:S(2)}) async-start(), calls=%async_computation.8 | async-start | bytes 1179648 | tf_op jit(solution)/shard_map/all_gather | solution.py:32
  8.0 10.1 %collective-permute-start = (f32[2,128]{1,0:T(2,128)S(1)}, f32[2,128]{1,0:T(2,128)S(1)}, u32[]{:S(2)}, u32[]{:S(2)}) collective-permute-start(f32[2,128]{1,0:T(2,128)S(1)} %bitcast.802), channel_id=1, source_target_pairs={{0,4},{4,8},{8,12},{12,16},{16,20},{20,24},{24,28},{28,32},{32,36}... | collective-permute-start | bytes 3080 | tf_op jit(solution)/shard_map/ppermute | solution.py:18
  18.1 3.4 copy-start.13
  18.1 3.4 copy-start.11
  138.8 9.3 %copy-start.12 = (f32[16,2,128]{2,1,0:T(2,128)}, f32[16,2,128]{2,1,0:T(2,128)S(1)}, u32[]{:S(2)}) copy-start(f32[16,2,128]{2,1,0:T(2,128)S(1)} %get-tuple-element.1423) | copy-start | bytes 49156
  143.0 3.1 copy-start.8
  148.1 157.3 %all-gather.23.cloned.1.call-start = ((), (), s32[]{:S(2)}) async-start(), calls=%async_computation.9 | async-start | bytes 1179648 | tf_op jit(solution)/shard_map/all_gather | solution.py:32
  148.1 2.4 copy-start.6
  148.1 26.3 %copy-start.7 = (f32[128,2,128]{0,2,1:T(8,128)S(1)}, f32[128,2,128]{0,2,1:T(8,128)}, u32[]{:S(2)}) copy-start(f32[128,2,128]{0,2,1:T(8,128)} %convolution_bitcast_fusion.24) | copy-start | bytes 393220
  171.3 2.1 copy-start.4
  184.7 16.2 %copy-start.3 = (f32[1024,2,128]{0,2,1:T(8,128)S(1)}, f32[1024,2,128]{0,2,1:T(8,128)}, u32[]{:S(2)}) copy-start(f32[1024,2,128]{0,2,1:T(8,128)} %all-gather.21.cloned.1.call-done) | copy-start | bytes 3145732
  201.5 22.3 %copy-start.16 = (f32[2,1,128]{2,1,0:T(1,128)S(1)}, f32[2,1,128]{2,1,0:T(1,128)}, u32[]{:S(2)}) copy-start(f32[2,1,128]{2,1,0:T(1,128)} %fusion.143) | copy-start | bytes 3076
  223.9 33.4 %copy-start.1 = (f32[2,256,128]{2,1,0:T(8,128)S(1)}, f32[2,256,128]{2,1,0:T(8,128)}, u32[]{:S(2)}) copy-start(f32[2,256,128]{2,1,0:T(8,128)} %param.25) | copy-start | bytes 786436
  257.3 3.7 copy-start.9
  257.5 34.3 %copy-start.15 = (f32[2,1,128]{2,1,0:T(1,128)S(1)}, f32[2,1,128]{2,1,0:T(1,128)}, u32[]{:S(2)}) copy-start(f32[2,1,128]{2,1,0:T(1,128)} %fusion.107) | copy-start | bytes 3076
  257.5 34.3 %copy-start.5 = (f32[256,2,128]{2,0,1:T(8,128)S(1)}, f32[256,2,128]{2,0,1:T(8,128)}, u32[]{:S(2)}) copy-start(f32[256,2,128]{2,0,1:T(8,128)} %copy-done.4) | copy-start | bytes 786436
  305.3 16.2 %copy-start.2 = (f32[1024,2,128]{0,2,1:T(8,128)S(1)}, f32[1024,2,128]{0,2,1:T(8,128)}, u32[]{:S(2)}) copy-start(f32[1024,2,128]{0,2,1:T(8,128)} %all-gather.23.cloned.1.call-done) | copy-start | bytes 3145732
  341.9 24.0 %copy-start.10 = (f32[2,256,128]{2,1,0:T(8,128)S(1)}, f32[2,256,128]{2,1,0:T(8,128)}, u32[]{:S(2)}) copy-start(f32[2,256,128]{2,1,0:T(8,128)} %get-tuple-element.912) | copy-start | bytes 786436
  341.9 24.1 %copy-start.14 = (f32[2,128]{1,0:T(2,128)S(1)}, f32[2,128]{1,0:T(2,128)}, u32[]{:S(2)}) copy-start(f32[2,128]{1,0:T(2,128)} %copy-done.13) | copy-start | bytes 3076
  386.0 14.0 %all-to-all-start.1 = ((f32[32,1,64]{2,1,0:T(1,128)}), f32[32,1,64]{2,1,0:T(1,128)S(1)}, u32[]{:S(2)}, u32[]{:S(2)}) async-start(f32[32,1,64]{2,1,0:T(1,128)} %bitcast.248), calls=%async_computation.1 | async-start | bytes 32768 | tf_op jit(solution)/shard_map/all_to_all | solution.py:56
  400.0 10.3 %all-to-all-start.4 = ((f32[8,32,128]{2,1,0:T(8,128)}), f32[8,32,128]{2,1,0:T(8,128)S(1)}, u32[]{:S(2)}, u32[]{:S(2)}) async-start(f32[8,32,128]{2,1,0:T(8,128)} %copy.195), calls=%async_computation.4 | async-start | bytes 262144 | tf_op jit(solution)/shard_map/all_to_all | solution.py:49
  411.0 12.4 %all-to-all-start.2 = ((f32[32,1,64]{2,1,0:T(1,128)}), f32[32,1,64]{2,1,0:T(1,128)S(1)}, u32[]{:S(2)}, u32[]{:S(2)}) async-start(f32[32,1,64]{2,1,0:T(1,128)} %broadcast_in_dim.116), calls=%async_computation.2 | async-start | bytes 32768 | tf_op jit(solution)/shard_map/all_to_all | solution.py:66
  423.4 12.4 %all-to-all-start.5 = ((f32[32,1,128]{2,1,0:T(1,128)}), f32[32,1,128]{2,1,0:T(1,128)S(1)}, u32[]{:S(2)}, u32[]{:S(2)}) async-start(f32[32,1,128]{2,1,0:T(1,128)} %bitcast.256), calls=%async_computation.5 | async-start | bytes 32768 | tf_op jit(solution)/shard_map/all_to_all | solution.py:56
  435.8 10.9 %all-to-all-start.3 = ((f32[8,1,2048]{2,1,0:T(1,128)}), f32[8,1,2048]{2,1,0:T(1,128)S(1)}, u32[]{:S(2)}, u32[]{:S(2)}) async-start(f32[8,1,2048]{2,1,0:T(1,128)} %reshape.378), calls=%async_computation.3 | async-start | bytes 131072 | tf_op jit(solution)/shard_map/all_to_all | solution.py:66
  447.4 12.4 %all-to-all-start.6 = ((f32[32,1,128]{2,1,0:T(1,128)}), f32[32,1,128]{2,1,0:T(1,128)S(1)}, u32[]{:S(2)}, u32[]{:S(2)}) async-start(f32[32,1,128]{2,1,0:T(1,128)} %broadcast_in_dim.119), calls=%async_computation.6 | async-start | bytes 32768 | tf_op jit(solution)/shard_map/all_to_all | solution.py:66
  460.5 10.0 %all-to-all-start.7 = ((f32[8,32,128]{2,1,0:T(8,128)}), f32[8,32,128]{2,1,0:T(8,128)S(1)}, u32[]{:S(2)}, u32[]{:S(2)}) async-start(f32[8,32,128]{2,1,0:T(8,128)} %broadcast_in_dim.121), calls=%async_computation.7 | async-start | bytes 262144 | tf_op jit(solution)/shard_map/all_to_all | solution.py:66
Sparse Core Ops, SparseCore 0:
  148.2 36.5 all-gather.20
  186.5 37.6 all-gather.22
where the time goes:
time: 483 us; the launch traced here: 478 us
  matrix products  164 us (34%)
  blocking collectives  100 us (21%)
  local copies, waits for them, and re-layouts  75.6 us (16%)
  waiting for transfers between devices  53.9 us (11%)
  starting transfers between devices  37.8 us (8%)
  other arithmetic  27.4 us (6%)
  between operations  14.9 us (3%)
    all_gather x10, blocking collectives, prefix_by_axis(): pieces = jax.tree.map(lambda part: lax.all_gather(part, axis), subtotal)  83.1 us
    dot_general x16, matrix products, compose(): jnp.dot(skew, maps.reshape(hidden, lane_count * hidden), precision=highest)  61.8 us
    while x96, local copies, waits for them, and re-layouts  30.2 us
    squeeze x32, local copies, waits for them, and re-layouts, on_device(): lax.scan(chain, (unit_stack, seq_zero), (blocks, offsets))  29.7 us
    dot_general x32, matrix products, advance(): moved = jnp.dot(state, skew_t, precision=highest) - damping * state  28.7 us
    all_to_all x4, waiting for transfers between devices, copy_for_each(): lax.all_to_all(jnp.broadcast_to(shard[None], (length, *shard.shape)), axi...  24.9 us
    dot_general x34, matrix products, join_maps(): jnp.einsum('isj,sj->si', later[0], earlier[1], precision=highest) + later[1]  22.9 us
    all_to_all x4, starting transfers between devices, copy_for_each(): lax.all_to_all(jnp.broadcast_to(shard[None], (length, *shard.shape)), axi...  18.5 us
  transfers between devices with their start and end apart: 10, of which 8 were waited for; matrix products, arithmetic and copies ran while one was open for 20% of the time, Pallas kernels for 0%

commit v1 on v0

v1 whole, which is shorter than its diff:
```python
import jax
import jax.numpy as jnp
from jax import lax
from jax.experimental import pallas as pl
from jax.experimental.pallas import tpu as pltpu
from jax.sharding import Mesh
from jax.sharding import PartitionSpec as P

H = 128
LEN = 16
TBLK = 128
AUG = 144
LANES = 12
GROUPS = 3
GROWS = LANES * H + 16
SEQ = ("x", "z", "core")
EULER = 0.02
F32 = jnp.float32
BF16 = jnp.bfloat16
MESH = pl.DeviceIdType.MESH
VM = pl.BlockSpec(memory_space=pltpu.VMEM)
SM = pl.BlockSpec(memory_space=pltpu.SMEM)


def split(value):
    high = value.astype(BF16)
    return high, (value - high.astype(F32)).astype(BF16)


def wide(value):
    return jnp.concatenate(split(value), axis=1)


def weights(matrix):
    row = wide(matrix)
    return jnp.concatenate([row, row], axis=0)


def times(rows, packed):
    both = jnp.dot(wide(rows), packed, preferred_element_type=F32)
    return both[:, :H] + both[:, H:]


def unit():
    line = lax.broadcasted_iota(jnp.int32, (H, H), 0)
    return jnp.where(line == lax.broadcasted_iota(jnp.int32, (H, H), 1), 1.0, 0.0).astype(F32)


def rate_matrix(weight, damping):
    return weight.T - weight - unit() * damping


def shift_down(block, first):
    line = lax.broadcasted_iota(jnp.int32, block.shape, 0)
    return jnp.where(line == 0, first, pltpu.roll(block, 1, 0))


def apply_rows(rows, packed_less_unit, offset):
    return rows + times(rows, packed_less_unit) + offset


def then(earlier, later, eye):
    tail = jnp.concatenate([jnp.zeros((H, H), F32), later[H:]], axis=0)
    return earlier + times(earlier, weights(later[:H] - eye)) + tail


def local_maps(
    x_ref, guess_ref, edge_ref, w_ref, damp_ref, u_ref, bias_ref, target_ref, steps_ref,
    gain_ref, resid_ref, maps_ref, prefix_ref, dev_ref, hit_ref,
):
    count = guess_ref.shape[0]
    steps = count // 2
    eye = unit()
    rate_t = rate_matrix(w_ref[...], damp_ref[...])
    packed = weights(rate_t)
    guess = guess_ref[...]
    prev = jnp.concatenate(
        [shift_down(guess[s * steps:(s + 1) * steps], edge_ref[s:s + 1, :]) for s in range(2)], axis=0
    )
    u_pair = wide(u_ref[...])
    x_high, x_low = split(x_ref[...])
    drive = jnp.dot(x_high, u_pair, preferred_element_type=F32)
    drive = drive + jnp.dot(x_low, u_pair, preferred_element_type=F32)
    preact = times(prev, packed) + drive[:, :H] + drive[:, H:] + bias_ref[...]
    activation = jnp.tanh(preact)
    gain_ref[0:count, :] = EULER * (1.0 - activation * activation)
    resid_ref[0:count, :] = prev + EULER * activation - guess
    line = lax.broadcasted_iota(jnp.int32, (LEN, H), 0)
    for s in range(2):
        for h in range(2):
            step = steps_ref[s, h]
            base = pl.multiple_of(s * steps + h * TBLK + (step // LEN) * LEN, LEN)
            kept = line <= lax.rem(step, LEN)
            to = pl.ds(count + (2 * s + h) * LEN, LEN)
            gain_ref[to, :] = jnp.where(kept, gain_ref[pl.ds(base, LEN), :], 0.0)
            resid_ref[to, :] = jnp.where(kept, resid_ref[pl.ds(base, LEN), :], 0.0)

    tail_pad = jnp.zeros((16 - LANES, H), F32)

    def group(g, carry):
        base = g * (LANES * LEN)

        def rows_at(ref, j):
            return [ref[pl.ds(base + i * LEN + j, 1), :] for i in range(LANES)]

        gains = rows_at(gain_ref, 0)
        for i in range(LANES):
            maps_ref[g, i * H:(i + 1) * H, :] = eye + rate_t * gains[i]
        maps_ref[g, LANES * H:, :] = jnp.concatenate(rows_at(resid_ref, 0) + [tail_pad], axis=0)

        def step(j, inner):
            gains = rows_at(gain_ref, j)
            for first in range(0, LANES, 4):
                last = first + 4
                end = last * H + (16 if last == LANES else 0)
                state = maps_ref[g, first * H:end, :]
                moved = times(state, packed)
                for i in range(4):
                    here = slice(i * H, (i + 1) * H)
                    maps_ref[g, (first + i) * H:(first + i + 1) * H, :] = (
                        state[here] + gains[first + i] * moved[here]
                    )
                if last == LANES:
                    more = jnp.concatenate(gains + [tail_pad], axis=0)
                    resid = jnp.concatenate(rows_at(resid_ref, j) + [tail_pad], axis=0)
                    maps_ref[g, LANES * H:, :] = state[4 * H:] + more * moved[4 * H:] + resid
            return inner

        return lax.fori_loop(1, LEN, step, carry)

    lax.fori_loop(0, GROUPS, group, 0)

    def lane_map(lane):
        g = lane // LANES
        i = lane - g * LANES
        begin = pl.multiple_of(i * H, H)
        return maps_ref[g, pl.ds(begin, H), :], maps_ref[g, pl.ds(LANES * H + i, 1), :]

    first_row = lax.broadcasted_iota(jnp.int32, (16, H), 0) == 0

    def chain(c, carry):
        out = []
        for s in range(2):
            run = carry[s]
            prefix_ref[s, c] = run
            main, offset = lane_map(s * (steps // LEN) + c)
            moved = run + times(run, weights(main - eye))
            last = moved[H:] + jnp.where(first_row, offset, 0.0)
            out.append(jnp.concatenate([moved[:H], last], axis=0))
        return tuple(out)

    start = jnp.concatenate([eye, jnp.zeros((16, H), F32)], axis=0)
    ends = lax.fori_loop(0, steps // LEN, chain, (start, start))
    for s in range(2):
        dev_ref[s] = ends[s]
        for h in range(2):
            step = steps_ref[s, h]
            c = h * (TBLK // LEN) + step // LEN
            main, offset = lane_map(2 * (steps // LEN) + 2 * s + h)
            run = prefix_ref[s, c]
            moved = run + times(run, weights(main - eye))
            here = guess_ref[pl.ds(s * steps + h * TBLK + step, 1), :]
            miss = offset + here - target_ref[2 * s + h:2 * s + h + 1, :]
            hit_ref[2 * s + h, 0:H, :] = moved[:H]
            hit_ref[2 * s + h, H:, :] = moved[H:] + jnp.where(first_row, miss, 0.0)


def shift_copy(src, dst, sends, recvs, target):
    return pltpu.make_async_remote_copy(
        src_ref=src, dst_ref=dst, send_sem=sends, recv_sem=recvs,
        device_id=target, device_id_type=MESH,
    )


def ring_gather(buf, axis, sends, recvs):
    n = lax.axis_size(axis)
    me = lax.axis_index(axis)
    half = AUG // 2
    sides = (lax.rem(me + 1, n), lax.rem(me + n - 1, n))
    started = []
    waiting = {}
    for k in range(1, n // 2 + 1):
        for side in range(2):
            slot = lax.rem(me + n - (k - 1), n) if side == 0 else lax.rem(me + k - 1, n)
            for piece in range(2) if k < n // 2 else (side,):
                if k > 1:
                    waiting[side, piece].wait_recv()
                part = buf.at[slot, pl.ds(piece * half, half)]
                copy = shift_copy(
                    part, part, sends.at[side, k - 1, piece], recvs.at[side, k - 1, piece], {axis: sides[side]}
                )
                copy.start()
                started.append(copy)
                waiting[side, piece] = copy
    for key in waiting:
        waiting[key].wait_recv()
    return started


def swap_all(buf, axis, sends, recvs):
    n = lax.axis_size(axis)
    me = lax.axis_index(axis)
    copies = [
        shift_copy(buf.at[me], buf.at[me], sends.at[d - 1], recvs.at[d - 1], {axis: lax.rem(me + d, n)})
        for d in range(1, n)
    ]
    for copy in copies:
        copy.start()
    for copy in copies:
        copy.wait_recv()
    return copies


def lane_sum(matrix):
    ones = jnp.ones((16, 2 * H), BF16)
    return lax.dot_general(ones, wide(matrix), (((1,), (1,)), ((), ())), preferred_element_type=F32)


def bridge(
    dev_ref, hit_ref, out_ref,
    pair, hits, zbuf, ubuf, xbuf, qz, qx, tiles, result,
    core_send, core_recv, zs, zr, xs, xr, vzs, vzr, vxs, vxr,
):
    x = lax.axis_index("x")
    z = lax.axis_index("z")
    c = lax.axis_index("core")
    nx = lax.axis_size("x")
    nz = lax.axis_size("z")
    other = 1 - c
    sibling = {"core": other}
    barrier = pltpu.get_barrier_semaphore()
    pl.semaphore_signal(barrier, inc=1, device_id=sibling, device_id_type=MESH)
    for d in range(1, nz):
        pl.semaphore_signal(barrier, inc=1, device_id={"z": lax.rem(z + d, nz)}, device_id_type=MESH)
    for d in range(1, nx):
        pl.semaphore_signal(barrier, inc=1, device_id={"x": lax.rem(x + d, nx)}, device_id_type=MESH)
    pl.semaphore_wait(barrier, nz + nx - 1)

    eye = unit()
    done = []
    first = shift_copy(dev_ref.at[other], pair.at[c], core_send.at[0], core_recv.at[0], sibling)
    first.start()
    second = shift_copy(
        hit_ref.at[pl.ds(2 * other, 2)], hits.at[c], core_send.at[1], core_recv.at[1], sibling
    )
    second.start()
    pair[c] = dev_ref[c]
    hits[c] = hit_ref[pl.ds(2 * c, 2)]
    first.wait_recv()
    zbuf[z] = then(pair[0], pair[1], eye)
    done += [first, second]
    done += ring_gather(zbuf, "z", zs, zr)
    second.wait_recv()

    start = jnp.concatenate([eye, jnp.zeros((16, H), F32)], axis=0)
    run = zbuf[0]
    ahead = start
    after = eye
    for k in range(1, nz):
        ahead = jnp.where(k == z, run, ahead)
        ubuf[k] = after
        element = zbuf[k]
        moved = times(jnp.concatenate([run, after], axis=0), weights(element[:H] - eye))
        run = run + moved[:AUG] + jnp.concatenate([jnp.zeros((H, H), F32), element[H:]], axis=0)
        after = jnp.where(k > z, after + moved[AUG:], after)
    xbuf[x] = run
    done += ring_gather(xbuf, "x", xs, xr)

    late = [then(pair[0], hits[1, h], eye) for h in range(2)]
    v = jnp.where(x > 0, xbuf[0, H:], 0.0)
    for k in range(1, nx - 1):
        v = jnp.where(k < x, apply_rows(v, weights(xbuf[k, :H] - eye), xbuf[k, H:]), v)
    v = apply_rows(v, weights(ahead[:H] - eye), ahead[H:])
    v_late = apply_rows(v, weights(pair[0, :H] - eye), pair[0, H:])
    q_late = jnp.zeros((16, H), F32)
    q = jnp.zeros((16, H), F32)
    scale = 0.125
    for h in range(2):
        miss = apply_rows(v, weights(hits[0, h, :H] - eye), hits[0, h, H:]) * scale
        q = q + times(miss, weights(hits[0, h, :H].T))
        miss = apply_rows(v, weights(late[h][:H] - eye), late[h][H:]) * scale
        q = q + times(miss, weights(late[h][:H].T))
        q_late = q_late + times(miss, weights(hits[1, h, :H].T))
    q_far = times(q, weights(ahead[:H].T))
    line = lax.broadcasted_iota(jnp.int32, (8, H), 0)
    qz[z] = jnp.where(line == 0, q[0:1], q_far[0:1])
    done += swap_all(qz, "z", vzs, vzr)
    total = jnp.zeros((H, H), F32)
    q_row = jnp.zeros((8, H), F32)
    for k in range(nz):
        if k > 0:
            total = total + jnp.where(k > z, ubuf[k] * qz[k, 0:1], 0.0)
        q_row = q_row + qz[k]
    near = lane_sum(total)
    qx[x] = q_row
    done += swap_all(qx, "x", vxs, vxr)
    t = jnp.where(nx - 1 > x, jnp.broadcast_to(qx[nx - 1, 1:2], (16, H)), 0.0)
    for k in range(nx - 2, 0, -1):
        moved = t + times(t, weights((xbuf[k, :H] - eye).T)) + qx[k, 1:2]
        t = jnp.where(k > x, moved, t)
    lam_late = near + t + times(t, weights((after - eye).T))
    lam = lam_late + times(lam_late, weights((pair[1, :H] - eye).T)) + q_late[0:1]
    early_tile = jnp.where(line == 0, v[0:1], lam[0:1])
    late_tile = jnp.where(line == 0, v_late[0:1], lam_late[0:1])
    result[c] = jnp.where(c == 0, early_tile, late_tile)
    tiles[...] = jnp.where(c == 0, late_tile, early_tile)
    final = shift_copy(tiles, result.at[c], core_send.at[2], core_recv.at[2], sibling)
    final.start()
    final.wait_recv()
    done.append(final)
    out_ref[...] = result[...]
    for copy in done:
        copy.wait_send()


def sweeps(
    x_ref, guess_ref, edge_ref, w_ref, damp_ref, target_ref, steps_ref, gain_ref, resid_ref,
    maps_ref, prefix_ref, hit_ref, ends_ref,
    traj_ref, grad_ref, start_ref, carry_ref, push_ref, source_ref, pre_ref,
):
    count = guess_ref.shape[0]
    steps = count // 2
    chunks = steps // LEN
    eye = unit()
    rate_t = rate_matrix(w_ref[...], damp_ref[...])
    packed = weights(rate_t)
    packed_t = weights(rate_t.T)
    push_ref[...] = jnp.zeros(push_ref.shape, F32)
    source_ref[...] = jnp.zeros(source_ref.shape, F32)

    def lane_map(lane):
        g = lane // LANES
        i = lane - g * LANES
        return maps_ref[g, pl.ds(pl.multiple_of(i * H, H), H), :]

    for s in range(2):
        column = jnp.broadcast_to(ends_ref[s, 0:1, :], (H, H)).T
        for k in range(chunks):
            start_ref[s * chunks + k:s * chunks + k + 1, :] = (
                jnp.sum(prefix_ref[s, k, :H, :] * column, axis=0, keepdims=True) + prefix_ref[s, k, H:H + 1, :]
            )
        for h in range(2):
            n = 2 * s + h
            step = steps_ref[s, h]
            miss = jnp.sum(hit_ref[n, :H, :] * column, axis=0, keepdims=True) + hit_ref[n, H:H + 1, :]
            miss = miss * 0.125
            source_ref[pl.ds(s * steps + h * TBLK + step, 1), :] = miss
            spread = jnp.broadcast_to(miss, (16, H))
            pushed = times(spread, weights(lane_map(2 * chunks + n).T))
            push_ref[pl.ds(s * chunks + h * (TBLK // LEN) + step // LEN, 1), :] = pushed[0:1]

    def back(i, carry):
        k = chunks - 1 - i
        out = []
        for s in range(2):
            t = carry[s]
            lane = s * chunks + k
            carry_ref[pl.ds(lane, 1), :] = t[0:1]
            moved = t + times(t, weights((lane_map(lane) - eye).T))
            out.append(moved + push_ref[pl.ds(lane, 1), :])
        return tuple(out)

    ends = tuple(jnp.broadcast_to(ends_ref[s, 1:2, :], (16, H)) for s in range(2))
    lax.fori_loop(0, chunks, back, ends)

    def sweep(j, carry):
        state, adjoint = carry
        ahead = pl.ds(j, 2 * chunks, stride=LEN)
        behind = pl.ds(LEN - 1 - j, 2 * chunks, stride=LEN)
        state = state + gain_ref[ahead, :] * times(state, packed) + resid_ref[ahead, :]
        traj_ref[ahead, :] = state + guess_ref[ahead, :]
        adjoint = adjoint + source_ref[behind, :]
        scaled = gain_ref[behind, :] * adjoint
        pre_ref[behind, :] = scaled
        return state, adjoint + times(scaled, packed_t)

    lax.fori_loop(0, LEN, sweep, (start_ref[...], carry_ref[...]))
    guess = guess_ref[...]
    prev = jnp.concatenate(
        [shift_down(guess[s * steps:(s + 1) * steps], edge_ref[s:s + 1, :]) for s in range(2)], axis=0
    )
    left_high, left_low = split(jnp.concatenate([prev, x_ref[...]], axis=1))
    right = wide(pre_ref[...])
    dims = (((0,), (0,)), ((), ()))
    both = lax.dot_general(left_high, right, dims, preferred_element_type=F32)
    both = both + lax.dot_general(left_low, right, dims, preferred_element_type=F32)
    grads = both[:, :H] + both[:, H:]
    grad_ref[0:H, :] = grads[:H].T - grads[:H]
    grad_ref[H:, :] = grads[H:]


def grad_sum(in_ref, out_ref, parts, shares, whole, send1, recv1, send2, recv2, send3, recv3):
    x = lax.axis_index("x")
    y = lax.axis_index("batch")
    z = lax.axis_index("z")
    c = lax.axis_index("core")
    nx, ny, nz, nc = (lax.axis_size(name) for name in ("x", "batch", "z", "core"))
    plane, column = nx * ny, nz * nc
    tiles = in_ref.shape[0] // plane
    p = x * ny + y
    q = z * nc + c
    planes = [lax.rem(p + d, plane) for d in range(1, plane)]
    columns = [lax.rem(q + d, column) for d in range(1, column)]
    plane_ids = [{"x": other // ny, "batch": lax.rem(other, ny)} for other in planes]
    column_ids = [{"z": other // nc, "core": lax.rem(other, nc)} for other in columns]
    barrier = pltpu.get_barrier_semaphore()
    for target in plane_ids + column_ids:
        pl.semaphore_signal(barrier, inc=1, device_id=target, device_id_type=MESH)
    pl.semaphore_wait(barrier, plane + column - 2)
    done = []
    for i in range(plane - 1):
        done.append(shift_copy(
            in_ref.at[pl.ds(planes[i] * tiles, tiles)], parts.at[p], send1.at[i], recv1.at[i], plane_ids[i]
        ))
        done[-1].start()
    parts[p] = in_ref[pl.ds(p * tiles, tiles)]
    for copy in done:
        copy.wait_recv()
    shares[q] = jnp.sum(parts[...], axis=0)
    exchange = [
        shift_copy(shares.at[q], shares.at[q], send2.at[i], recv2.at[i], column_ids[i])
        for i in range(column - 1)
    ]
    for copy in exchange:
        copy.start()
    for copy in exchange:
        copy.wait_recv()
    mine = pl.ds(p * tiles, tiles)
    whole[mine] = jnp.sum(shares[...], axis=0)
    last = [
        shift_copy(whole.at[mine], whole.at[mine], send3.at[i], recv3.at[i], plane_ids[i])
        for i in range(plane - 1)
    ]
    for copy in last:
        copy.start()
    for copy in last:
        copy.wait_recv()
    out_ref[...] = whole[...]
    for copy in done + exchange + last:
        copy.wait_send()


def vmem(*dims):
    return pltpu.VMEM(dims, F32)


def out(*dims):
    return jax.ShapeDtypeStruct(dims, F32)


def on_device(inputs, guess_path, recur_weight, damping, in_weight, bias_term, targets, target_steps):
    seqs, steps, hidden = guess_path.shape
    count = seqs * steps
    chunks = steps // LEN
    nx, nz, nc, ny = (lax.axis_size(name) for name in ("x", "z", "core", "batch"))
    devices = nx * nz * nc
    edge = lax.ppermute(guess_path[:, steps - 1, :], SEQ, [(i, i + 1) for i in range(devices - 1)])
    x = inputs.reshape(count, -1)
    guess = guess_path.reshape(count, hidden)
    damp = damping.reshape(1, hidden)
    target = targets.reshape(-1, hidden)
    extra = count + 4 * LEN
    big = pltpu.CompilerParams(vmem_limit_bytes=48 * 1024 * 1024)
    gain, resid, maps, prefix, dev, hit = pl.pallas_call(
        local_maps,
        out_shape=(
            out(extra, hidden), out(extra, hidden), out(GROUPS, GROWS, hidden),
            out(seqs, chunks, AUG, hidden), out(seqs, AUG, hidden), out(2 * seqs, AUG, hidden),
        ),
        in_specs=[VM] * 8 + [SM],
        out_specs=[VM] * 6,
        compiler_params=big,
        name="local_maps",
    )(x, guess, edge, recur_weight, damp, in_weight, bias_term.reshape(1, hidden), target, target_steps)
    dma = pltpu.SemaphoreType.DMA
    ends = pl.pallas_call(
        bridge,
        out_shape=out(seqs, 8, hidden),
        in_specs=[VM] * 2,
        out_specs=VM,
        scratch_shapes=[
            vmem(2, AUG, hidden), vmem(2, 2, AUG, hidden), vmem(nz, AUG, hidden), vmem(nz, hidden, hidden),
            vmem(nx, AUG, hidden), vmem(nz, 8, hidden), vmem(nx, 8, hidden), vmem(8, hidden), vmem(2, 8, hidden),
            dma((3,)), dma((3,)), dma((2, nz // 2, 2)), dma((2, nz // 2, 2)), dma((2, nx // 2, 2)),
            dma((2, nx // 2, 2)), dma((nz - 1,)), dma((nz - 1,)), dma((nx - 1,)), dma((nx - 1,)),
        ],
        compiler_params=pltpu.CompilerParams(
            collective_id=0, has_side_effects=True, vmem_limit_bytes=32 * 1024 * 1024
        ),
        name="bridge",
    )(dev, hit)
    traj, grads = pl.pallas_call(
        sweeps,
        out_shape=(out(count, hidden), out(3 * hidden, hidden)),
        in_specs=[VM] * 6 + [SM] + [VM] * 6,
        out_specs=[VM] * 2,
        scratch_shapes=[
            vmem(2 * chunks, hidden), vmem(2 * chunks, hidden), vmem(2 * chunks, hidden),
            vmem(count, hidden), vmem(count, hidden),
        ],
        compiler_params=big,
        name="sweeps",
    )(x, guess, edge, recur_weight, damp, target, target_steps, gain, resid, maps, prefix, hit, ends)
    plane, column = nx * ny, nz * nc
    tiles = 3 * hidden // 8 // plane
    whole = pl.pallas_call(
        grad_sum,
        out_shape=out(3 * hidden // 8, 8, hidden),
        in_specs=[VM],
        out_specs=VM,
        scratch_shapes=[
            vmem(plane, tiles, 8, hidden), vmem(column, tiles, 8, hidden), vmem(3 * hidden // 8, 8, hidden),
            dma((plane - 1,)), dma((plane - 1,)), dma((column - 1,)), dma((column - 1,)),
            dma((plane - 1,)), dma((plane - 1,)),
        ],
        compiler_params=pltpu.CompilerParams(
            collective_id=1, has_side_effects=True, vmem_limit_bytes=16 * 1024 * 1024
        ),
        name="grad_sum",
    )(grads.reshape(-1, 8, hidden))
    whole = whole.reshape(3 * hidden, hidden)
    return traj.reshape(guess_path.shape), whole[:hidden], whole[hidden:]


def solution(mesh):
    torus = Mesh(mesh.devices.reshape(4, 8, 2, mesh.shape["batch"]), (*SEQ, "batch"))
    return jax.shard_map(
        on_device,
        mesh=torus,
        in_specs=(
            P("batch", SEQ, None), P("batch", SEQ, None), P(), P(), P(), P(), P("batch", SEQ, None), P("batch", SEQ),
        ),
        out_specs=(P("batch", SEQ, None), P(), P()),
        check_vma=False,
    )
```

time: 483 us -> 114 us (0.24)
  matrix products: 164 us -> 0 us
  blocking collectives: 100 us -> 0 us
  Pallas kernels: 0 us -> 98.6 us
  local copies, waits for them, and re-layouts: 75.6 us -> 8.4 us
  waiting for transfers between devices: 53.9 us -> 0.7 us
  starting transfers between devices: 37.8 us -> 4.91 us
  other arithmetic: 27.4 us -> 0 us
  between operations: 14.9 us -> 0.66 us
    dot_general x222 -> x0, matrix products: 164 us -> none  [the longest x16 61.8 us: compose(): jnp.dot(skew, maps.reshape(hidden, lane_count * hidden), precision=highest)]
    pallas_call x0 -> x4, Pallas kernels: none -> 98.6 us  [the longest x1 43.3 us: on_device(): pl.pallas_call(bridge, out_shape=out(seqs, 8, hidden), in_specs=[VM] * 2,...]
    all_gather x10 -> x0, blocking collectives: 83.1 us -> none  [prefix_by_axis(): pieces = jax.tree.map(lambda part: lax.all_gather(part, axis), subtotal)]
    all_to_all x7 -> x0, waiting for transfers between devices: 45.1 us -> none  [the longest x4 24.9 us: copy_for_each(): lax.all_to_all(jnp.broadcast_to(shard[None], (length, *shard.shape)), axi...]
    all_to_all x7 -> x0, starting transfers between devices: 32.9 us -> none  [the longest x4 18.5 us: copy_for_each(): lax.all_to_all(jnp.broadcast_to(shard[None], (length, *shard.shape)), axi...]
    while x97 -> x0, local copies, waits for them, and re-layouts: 31 us -> none
    squeeze x32 -> x0, local copies, waits for them, and re-layouts: 29.7 us -> none  [on_device(): lax.scan(chain, (unit_stack, seq_zero), (blocks, offsets))]
    add x89 -> x0, other arithmetic: 21 us -> none  [the longest x48 11.4 us: apply_map(): jnp.einsum('isj,sj->si', block_map, carry, precision=lax.Precision.HIGHEST)]
  transfers between devices with their start and end apart: 10 -> 1, of which waited for: 8 -> 1; matrix products, arithmetic and copies ran while one was open for 20% -> 0% of each run, Pallas kernels for 0% -> 0%
where the time goes in v1:
time: 114 us; the launch traced here: 113 us
  Pallas kernels  98.6 us (86%)
  local copies, waits for them, and re-layouts  8.4 us (7%)
  starting transfers between devices  4.91 us (4%)
    pallas_call x1, Pallas kernels, on_device(): pl.pallas_call(bridge, out_shape=out(seqs, 8, hidden), in_specs=[VM] * 2,...  43.3 us
    pallas_call x1, Pallas kernels, on_device(): pl.pallas_call(local_maps, out_shape=(out(extra, hidden), out(extra, hidd...  24 us
    pallas_call x1, Pallas kernels, on_device(): pl.pallas_call(grad_sum, out_shape=out(3 * hidden // 8, 8, hidden), in_sp...  21.6 us
    pallas_call x1, Pallas kernels, on_device(): pl.pallas_call(sweeps, out_shape=(out(count, hidden), out(3 * hidden, hid...  9.76 us
    unnamed x16, local copies, waits for them, and re-layouts  6.4 us
    ppermute x1, starting transfers between devices, on_device(): lax.ppermute(guess_path[:, steps - 1, :], SEQ, [(i, i + 1) for i in range...  4.91 us
  transfers between devices with their start and end apart: 1, of which 1 were waited for; matrix products, arithmetic and copies ran while one was open for 0% of the time, Pallas kernels for 0%

profile of v1, /device:TPU:1, one launch (start us, length us, event | category | flops | bytes accessed | tf_op | source)
XLA Modules:
  0.0 113.3 jit_solution(16365187295817245502)
XLA Ops:
  0.6 0.7 slice.15
  1.3 4.9 %collective-permute-start = (f32[2,128]{1,0:T(2,128)S(1)}, f32[2,128]{1,0:T(2,128)S(1)}, u32[]{:S(2)}, u32[]{:S(2)}) collective-permute-start(f32[2,128]{1,0:T(2,128)S(1)} %bitcast.24), channel_id=1, source_target_pairs={{0,4},{4,8},{8,12},{12,16},{16,20},{20,24},{24,28},{28,32},{32,36}... | collective-permute-start | bytes 3080 | tf_op jit(solution)/shard_map/ppermute | solution.py:457
  6.3 0.7 collective-permute-done.edge_ref
  7.0 0.0 copy-start
  7.0 1.0 copy-done
  8.0 0.0 copy-start.1
  8.0 0.9 copy-done.1
  8.9 0.0 copy-start.2
  9.0 0.8 copy-done.2
  9.8 0.0 copy-start.3
  9.8 0.9 copy-done.3
  10.7 0.0 copy-start.4
  10.7 0.7 copy-done.4
  11.4 0.0 copy-start.5
  11.4 0.7 copy-done.5
  12.1 0.0 copy-start.6
  12.1 0.7 copy-done.6
  12.7 0.0 copy-start.7
  12.7 0.7 copy-done.7
  13.4 24.0 %local_maps.1 = (f32[576,128]{1,0:T(8,128)S(1)}, f32[576,128]{1,0:T(8,128)S(1)}, f32[3,1552,128]{2,1,0:T(8,128)}, f32[2,16,144,128]{3,2,1,0:T(8,128)S(1)}, f32[2...) custom-call(f32[512,256]{1,0:T(8,128)S(1)} %bitcast.14, f32[512,128]{1,0:T(8,128)S(1)} %bitcast.16, ...), custom_call_target="tpu_custom_call" | custom-call | tf_op jit(solution)/shard_map/local_maps/pallas_call | solution.py:464
  37.4 43.3 %bridge.1.ends_ref = f32[2,8,128]{2,1,0:T(8,128)S(1)} custom-call(f32[2,144,128]{2,1,0:T(8,128)S(1)} %get-tuple-element.16.dev_ref, f32[4,144,128]{2,1,0:T(8,128)S(1)} %get-tuple-element.15.hit_ref), custom_call_target="tpu_custom_call" | custom-call | tf_op jit(solution)/shard_map/bridge/pallas_call | solution.py:476
  80.7 9.8 %sweeps.1 = (f32[512,128]{1,0:T(8,128)}, f32[384,128]{1,0:T(8,128)S(1)}) custom-call(f32[512,256]{1,0:T(8,128)S(1)} %bitcast.15, f32[512,128]{1,0:T(8,128)S(1)} %bitcast.17, f32[2,128]{1,0:T(2,128)S(1)} %collective-permute-done.edge_ref, f32[128,128]{1,0:T(8,128)S(1)} %copy-done.2, f32[1,128]{1,0:T(1,128)S(1)} %bitcast.22, f32[4,128]{1,0:T(4,128)S(1)} %bitcast.20, ...), custom_call_target="tpu_custom_call" | custom-call | tf_op jit(solution)/shard_map/sweeps/pallas_call | solution.py:492
  90.4 21.6 %grad_sum.1 = f32[48,8,128]{2,1,0:T(8,128)S(1)} custom-call(f32[48,8,128]{2,1,0:T(8,128)S(1)} %bitcast.18), custom_call_target="tpu_custom_call" | custom-call | tf_op jit(solution)/shard_map/grad_sum/pallas_call | solution.py:506
  112.0 0.6 slice_bitcast_fusion.1
  112.6 0.7 slice_bitcast_fusion
Async XLA Ops:
  1.3 5.6 %collective-permute-start = (f32[2,128]{1,0:T(2,128)S(1)}, f32[2,128]{1,0:T(2,128)S(1)}, u32[]{:S(2)}, u32[]{:S(2)}) collective-permute-start(f32[2,128]{1,0:T(2,128)S(1)} %bitcast.24), channel_id=1, source_target_pairs={{0,4},{4,8},{8,12},{12,16},{16,20},{20,24},{24,28},{28,32},{32,36}... | collective-permute-start | bytes 3080 | tf_op jit(solution)/shard_map/ppermute | solution.py:457
  7.0 1.0 copy-start
  8.0 0.9 copy-start.1
  8.9 0.8 copy-start.2
  9.8 0.9 copy-start.3
  10.7 0.7 copy-start.4
  11.4 0.7 copy-start.5
  12.1 0.7 copy-start.6
  12.7 0.7 copy-start.7

commit v2 on v0

v2 whole, which is shorter than its diff:
```python
import jax
import jax.numpy as jnp
from jax import lax
from jax.experimental import pallas as pl
from jax.experimental.pallas import tpu as pltpu
from jax.sharding import Mesh
from jax.sharding import PartitionSpec as P

H = 128
LEN = 16
TBLK = 128
AUG = 144
SENT = 136
SEQ = ("x", "z", "core")
EULER = 0.02
F32 = jnp.float32
BF16 = jnp.bfloat16
MESH = pl.DeviceIdType.MESH
VM = pl.BlockSpec(memory_space=pltpu.VMEM)
HBM = pl.BlockSpec(memory_space=pl.ANY)


def split(value):
    high = value.astype(BF16)
    return high, (value - high.astype(F32)).astype(BF16)


def wide(value):
    return jnp.concatenate(split(value), axis=1)


def weights(matrix):
    row = wide(matrix)
    return jnp.concatenate([row, row], axis=0)


def times(rows, packed):
    both = jnp.dot(wide(rows), packed, preferred_element_type=F32)
    return both[:, :H] + both[:, H:]


def unit():
    line = lax.broadcasted_iota(jnp.int32, (H, H), 0)
    return jnp.where(line == lax.broadcasted_iota(jnp.int32, (H, H), 1), 1.0, 0.0).astype(F32)


def rate_matrix(weight, damping):
    return weight.T - weight - unit() * damping


def shift_down(block, first):
    line = lax.broadcasted_iota(jnp.int32, block.shape, 0)
    return jnp.where(line == 0, first, pltpu.roll(block, 1, 0))


def tail_of(rows):
    return jnp.concatenate([rows, jnp.zeros((8, H), F32)], axis=0)


def then(earlier, later, offset, eye):
    moved = earlier + times(earlier, weights(later - eye))
    return jnp.concatenate([moved[:H], moved[H:] + offset], axis=0)


def remote(src, dst, sends, recvs, target):
    return pltpu.make_async_remote_copy(
        src_ref=src, dst_ref=dst, send_sem=sends, recv_sem=recvs,
        device_id=target, device_id_type=MESH,
    )


def swap_copies(buf, axis, sends, recvs, rows):
    n = lax.axis_size(axis)
    me = lax.axis_index(axis)
    part = buf.at[me, pl.ds(0, rows)]
    return [
        remote(part, part, sends.at[d - 1], recvs.at[d - 1], {axis: lax.rem(me + d, n)}) for d in range(1, n)
    ]


def lane_sum(matrix):
    ones = jnp.ones((16, 2 * H), BF16)
    return lax.dot_general(ones, wide(matrix), (((1,), (1,)), ((), ())), preferred_element_type=F32)


def newton(
    x_hbm, guess_hbm, w_hbm, damp_hbm, u_hbm, bias_hbm, target_hbm, steps_hbm,
    traj_hbm, recur_ref, gin_ref,
    x_ref, guess_ref, w_ref, damp_ref, u_ref, bias_ref, target_ref, steps_ref, load_sem,
    edge, gain_ref, resid_ref, offs_ref, maps_ref, tree, totals, prefix, suffix, turned,
    pair, hit_ref, hits, zbuf, ubuf, xbuf, qz, qx, tiles, ends,
    start_ref, carry_ref, push_ref, source_ref, pre_ref, traj_ref,
    grads, parts, shares, whole,
    edge_send, edge_recv, core_send, core_recv, zs, zr, xs, xr, vzs, vzr, vxs, vxr,
    send1, recv1, send2, recv2, send3, recv3,
):
    x, y, z, c = (lax.axis_index(name) for name in ("x", "batch", "z", "core"))
    nx, ny, nz, nc = (lax.axis_size(name) for name in ("x", "batch", "z", "core"))
    count = guess_ref.shape[0]
    steps = count // 2
    chunks = steps // LEN
    lanes = 2 * chunks
    blocks = TBLK // LEN

    loads = [
        pltpu.make_async_copy(src, dst, load_sem.at[i])
        for i, (src, dst) in enumerate((
            (w_hbm, w_ref), (damp_hbm, damp_ref), (guess_hbm, guess_ref), (u_hbm, u_ref), (x_hbm, x_ref),
            (bias_hbm, bias_ref), (target_hbm, target_ref), (steps_hbm, steps_ref),
        ))
    ]
    for load in loads:
        load.start()

    other = 1 - c
    sibling = {"core": other}
    plane, column = nx * ny, nz * nc
    p = x * ny + y
    q = z * nc + c
    planes = [lax.rem(p + d, plane) for d in range(1, plane)]
    columns = [lax.rem(q + d, column) for d in range(1, column)]
    plane_ids = [{"x": mate // ny, "batch": lax.rem(mate, ny)} for mate in planes]
    column_ids = [{"z": mate // nc, "core": lax.rem(mate, nc)} for mate in columns]
    place = x * column + q

    def along(where):
        return {"x": where // column, "z": lax.rem(where // nc, nz), "core": lax.rem(where, nc)}

    following = along(lax.rem(place + 1, nx * column))
    preceding = along(lax.rem(place + nx * column - 1, nx * column))
    barrier = pltpu.get_barrier_semaphore()
    greeted = plane_ids + column_ids + [following, preceding]
    for target in greeted:
        pl.semaphore_signal(barrier, inc=1, device_id=target, device_id_type=MESH)

    eye = unit()
    loads[0].wait()
    loads[1].wait()
    rate_t = rate_matrix(w_ref[...], damp_ref[...])
    packed = weights(rate_t)
    for load in loads[2:]:
        load.wait()
    guess = guess_ref[...]

    def prev_rows(firsts):
        return jnp.concatenate(
            [shift_down(guess_ref[s * steps:(s + 1) * steps, :], firsts[s]) for s in range(2)], axis=0
        )

    zero_row = jnp.zeros((1, H), F32)
    u_pair = wide(u_ref[...])
    x_high, x_low = split(x_ref[...])
    drive = jnp.dot(x_high, u_pair, preferred_element_type=F32)
    drive = drive + jnp.dot(x_low, u_pair, preferred_element_type=F32)
    prev = prev_rows([zero_row, zero_row])
    preact = times(prev, packed) + drive[:, :H] + drive[:, H:] + bias_ref[...]
    activation = jnp.tanh(preact)
    gain_ref[0:count, :] = EULER * (1.0 - activation * activation)
    resid_ref[0:count, :] = prev + EULER * activation - guess
    early_preact = [preact[s * steps:s * steps + 1] for s in range(2)]

    pl.semaphore_wait(barrier, len(greeted))
    edge_copies = [
        remote(guess_ref.at[pl.ds((s + 1) * steps - 8, 8)], edge.at[s], edge_send.at[s], edge_recv.at[s], following)
        for s in range(2)
    ]
    for copy in edge_copies:
        copy.start()

    chunk_line = lax.broadcasted_iota(jnp.int32, (LEN, H), 0)

    def begin(s):
        gains = jnp.where(chunk_line == 0, 0.0, gain_ref[pl.ds(s * steps, chunks, stride=LEN), :])
        for k in range(chunks):
            maps_ref[s * chunks + k] = eye + rate_t * gains[k:k + 1]
        offs_ref[s * chunks:(s + 1) * chunks, :] = jnp.where(
            chunk_line == 0, 0.0, resid_ref[pl.ds(s * steps, chunks, stride=LEN), :]
        )

    def step_maps(base, size, gains, resid):
        for first in range(0, size, 4):
            state = maps_ref[base + first:base + first + 4].reshape(4 * H, H)
            if first + 4 == size:
                state = jnp.concatenate([state, offs_ref[base:base + 16, :]], axis=0)
            moved = times(state, packed)
            for i in range(4):
                here = slice(i * H, (i + 1) * H)
                maps_ref[base + first + i] = state[here] + gains[first + i:first + i + 1] * moved[here]
            if first + 4 == size:
                offs_ref[base:base + 16, :] = state[4 * H:] + gains * moved[4 * H:] + resid

    def compose(s, begin_at, end_at):
        def body(i, carry):
            for u in range(3):
                j = 1 + 3 * i + u
                rows = pl.ds(s * steps + j, chunks, stride=LEN)
                step_maps(s * chunks, chunks, gain_ref[rows, :], resid_ref[rows, :])
            return carry

        lax.fori_loop(begin_at, end_at, body, 0)

    first_row = chunk_line == 0

    def offset_of(lane):
        return jnp.where(first_row, offs_ref[pl.ds(lane, 1), :], 0.0)

    def lane_rows(lane):
        return jnp.concatenate([maps_ref[lane], offset_of(lane)], axis=0)

    def finish(s):
        lane = s * chunks
        gain = gain_ref[s * steps:s * steps + 1, :]
        resid = jnp.where(first_row, resid_ref[s * steps:s * steps + 1, :], 0.0)
        step = jnp.concatenate([eye + rate_t * gain, resid], axis=0)
        whole_chunk = then(step, maps_ref[lane], offset_of(lane), eye)
        maps_ref[lane] = whole_chunk[:H]
        offs_ref[lane:lane + 1, :] = whole_chunk[H:H + 1]
        for k in range(chunks // 2):
            tree[k] = then(lane_rows(lane + 2 * k), maps_ref[lane + 2 * k + 1], offset_of(lane + 2 * k + 1), eye)
        size = chunks // 2
        while size > 1:
            for k in range(size // 2):
                joined = then(tree[2 * k], tree[2 * k + 1, :H, :], tree[2 * k + 1, H:, :], eye)
                if size == 2:
                    totals[s] = joined
                else:
                    tree[k] = joined
            size //= 2

    core_copy = remote(
        totals.at[other, pl.ds(0, SENT)], pair.at[c, pl.ds(0, SENT)], core_send.at[0], core_recv.at[0], sibling
    )
    z_copies = swap_copies(zbuf, "z", zs, zr, SENT)

    def leave():
        core_copy.wait_recv()
        pair[c] = totals[c]
        zbuf[z] = then(
            jnp.concatenate([pair[0, :H, :], tail_of(pair[0, H:SENT, :])], axis=0),
            pair[1, :H, :], tail_of(pair[1, H:SENT, :]), eye,
        )
        for copy in z_copies:
            copy.start()

    begin(0)
    begin(1)
    compose(0, 0, (LEN - 1) // 3)
    for copy in edge_copies:
        copy.wait_recv()
    at_start = jnp.where(place > 0, 1.0, 0.0)
    firsts = [edge[s, 7:8, :] * at_start for s in range(2)]
    added = times(jnp.concatenate(firsts + [jnp.zeros((14, H), F32)], axis=0), packed)
    for s in range(2):
        row = slice(s * steps, s * steps + 1)
        activation = jnp.tanh(early_preact[s] + added[s:s + 1])
        gain_ref[row, :] = EULER * (1.0 - activation * activation)
        resid_ref[row, :] = firsts[s] + EULER * activation - guess_ref[row, :]
    finish(0)

    @pl.when(c == 1)
    def _():
        core_copy.start()

    compose(1, 0, 2)

    @pl.when(c == 0)
    def _():
        leave()

    compose(1, 2, (LEN - 1) // 3)
    finish(1)

    @pl.when(c == 0)
    def _():
        core_copy.start()

    for s in range(2):
        for h in range(2):
            n = 2 * s + h
            step = steps_ref[s, h]
            kept = chunk_line <= lax.rem(step, LEN)
            to = slice(count + n * LEN, count + (n + 1) * LEN)
            for ref in (gain_ref, resid_ref):
                rows = jnp.zeros((LEN, H), F32)
                for k in range(blocks):
                    base = s * steps + h * TBLK + k * LEN
                    rows = jnp.where(chunk_line * 0 + step // LEN == k, ref[base:base + LEN, :], rows)
                ref[to, :] = jnp.where(kept, rows, 0.0)
    hit_pad = jnp.zeros((12, H), F32)

    def hit_rows(ref, j):
        return jnp.concatenate([ref[pl.ds(count + j, 4, stride=LEN), :], hit_pad], axis=0)

    gains = hit_rows(gain_ref, 0)
    for n in range(4):
        maps_ref[lanes + n] = eye + rate_t * gains[n:n + 1]
    offs_ref[lanes:lanes + 16, :] = hit_rows(resid_ref, 0)

    def compose_hits(begin_at, end_at):
        def body(i, carry):
            for u in range(3):
                j = 1 + 3 * i + u
                step_maps(lanes, 4, hit_rows(gain_ref, j), hit_rows(resid_ref, j))
            return carry

        lax.fori_loop(begin_at, end_at, body, 0)

    compose_hits(0, 2)

    @pl.when(c == 1)
    def _():
        leave()

    compose_hits(2, (LEN - 1) // 3)

    start = jnp.concatenate([eye, jnp.zeros((16, H), F32)], axis=0)

    def chain(k, carry):
        out = []
        for s in range(2):
            lane = s * chunks + k
            prefix[lane] = carry[s]
            out.append(then(carry[s], maps_ref[lane], offset_of(lane), eye))
        return tuple(out)

    lax.fori_loop(0, chunks, chain, (start, start))
    block_line = lax.broadcasted_iota(jnp.int32, (TBLK, H), 0)
    map_line = jnp.zeros((AUG, H), jnp.int32)
    for s in range(2):
        for h in range(2):
            n = 2 * s + h
            step = steps_ref[s, h]
            run = jnp.zeros((AUG, H), F32)
            for k in range(blocks):
                run = jnp.where(map_line + step // LEN == k, prefix[s * chunks + h * blocks + k], run)
            base = s * steps + h * TBLK
            here = jnp.where(block_line == step, guess_ref[base:base + TBLK, :], 0.0)
            miss = offs_ref[lanes + n:lanes + n + 1, :] + jnp.sum(here, axis=0, keepdims=True)
            miss = miss - target_ref[n:n + 1, :]
            hit_ref[n] = then(run, maps_ref[lanes + n], jnp.where(first_row, miss, 0.0), eye)
    hit_copy = remote(
        hit_ref.at[pl.ds(2 * other, 2)], hits.at[c], core_send.at[1], core_recv.at[1], sibling
    )
    hit_copy.start()
    hits[c] = hit_ref[pl.ds(2 * c, 2)]

    def back_chain(i, carry):
        k = chunks - 1 - i
        out = []
        for s in range(2):
            lane = s * chunks + k
            suffix[lane] = carry[s]
            turn = weights((maps_ref[lane] - eye).T)
            turned[lane] = turn
            out.append(carry[s] + times(carry[s], turn))
        return tuple(out)

    lax.fori_loop(0, chunks, back_chain, (eye, eye))

    for copy in z_copies:
        copy.wait_recv()
    run = jnp.concatenate([zbuf[0, :H, :], tail_of(zbuf[0, H:SENT, :])], axis=0)
    ahead = start
    after = eye
    for k in range(1, nz):
        ahead = jnp.where(k == z, run, ahead)
        ubuf[k] = after
        moved = times(jnp.concatenate([run, after], axis=0), weights(zbuf[k, :H, :] - eye))
        offset = tail_of(zbuf[k, H:SENT, :])
        run = run + moved[:AUG] + jnp.concatenate([jnp.zeros((H, H), F32), offset], axis=0)
        after = jnp.where(k > z, after + moved[AUG:], after)
    xbuf[x] = run
    inner = jnp.logical_and(x > 0, x < nx - 1)

    def x_copy(slot, full, d):
        part = xbuf.at[slot, pl.ds(0, SENT) if full else pl.ds(H, 8)]
        return remote(part, part, xs.at[d - 1], xr.at[d - 1], {"x": lax.rem(x + d, nx)})

    def x_copies(slot, full):
        return [x_copy(slot, full, d) for d in range(1, nx)]

    @pl.when(inner)
    def _():
        for copy in x_copies(x, True):
            copy.start()

    @pl.when(jnp.logical_not(inner))
    def _():
        for copy in x_copies(x, False):
            copy.start()

    hit_copy.wait_recv()
    first_map = jnp.concatenate([pair[0, :H, :], tail_of(pair[0, H:SENT, :])], axis=0)
    late = [then(first_map, hits[1, h, :H, :], hits[1, h, H:, :], eye) for h in range(2)]
    w_ahead = weights(ahead[:H] - eye)
    w_first = weights(pair[0, :H, :] - eye)
    w_hits = [weights(hits[0, h, :H, :] - eye) for h in range(2)] + [weights(late[h][:H] - eye) for h in range(2)]
    t_hits = [weights(hits[0, h, :H, :].T) for h in range(2)] + [weights(late[h][:H].T) for h in range(2)]
    t_late = [weights(hits[1, h, :H, :].T) for h in range(2)]
    t_ahead = weights(ahead[:H].T)
    miss_rows = [hits[0, h, H:, :] for h in range(2)] + [late[h][H:] for h in range(2)]

    for d in range(1, nx):
        source = lax.rem(x + nx - d, nx)
        source_inner = jnp.logical_and(source > 0, source < nx - 1)

        @pl.when(source_inner)
        def _():
            x_copy(source, True, d).wait_recv()

        @pl.when(jnp.logical_not(source_inner))
        def _():
            x_copy(source, False, d).wait_recv()

    v = jnp.where(x > 0, tail_of(xbuf[0, H:SENT, :]), 0.0)
    for k in range(1, nx - 1):
        moved = v + times(v, weights(xbuf[k, :H, :] - eye)) + tail_of(xbuf[k, H:SENT, :])
        v = jnp.where(k < x, moved, v)
    v = v + times(v, w_ahead) + ahead[H:]
    scale = 0.125
    misses = [(v + times(v, w_hits[i]) + miss_rows[i]) * scale for i in range(4)]
    pull = jnp.zeros((16, H), F32)
    for i in range(4):
        pull = pull + times(misses[i], t_hits[i])
    far = times(pull, t_ahead)
    line = lax.broadcasted_iota(jnp.int32, (8, H), 0)
    qz[z] = jnp.where(line == 0, pull[0:1], far[0:1])
    vz_copies = swap_copies(qz, "z", vzs, vzr, 8)
    for copy in vz_copies:
        copy.start()
    v_late = v + times(v, w_first) + tail_of(pair[0, H:SENT, :])
    ends[0, c] = jnp.where(c == 0, v[:8], v_late[:8])
    tiles[0] = jnp.where(c == 0, v_late[:8], v[:8])
    delta_copy = remote(tiles.at[0], ends.at[0, c], core_send.at[2], core_recv.at[2], sibling)
    delta_copy.start()
    pull_late = times(misses[2], t_late[0]) + times(misses[3], t_late[1])
    delta_copy.wait_recv()

    lane_line = lax.broadcasted_iota(jnp.int32, (lanes, H), 0)
    pushes = jnp.zeros((lanes, H), F32)
    columns_d = [jnp.broadcast_to(ends[0, s, 0:1, :], (H, H)).T for s in range(2)]
    for s in range(2):
        for h in range(2):
            n = 2 * s + h
            step = steps_ref[s, h]
            miss = jnp.sum(hit_ref[n, :H, :] * columns_d[s], axis=0, keepdims=True) + hit_ref[n, H:H + 1, :]
            miss = miss * scale
            source_ref[s * steps + h * TBLK:s * steps + (h + 1) * TBLK, :] = jnp.where(block_line == step, miss, 0.0)
            pushed = times(jnp.broadcast_to(miss, (16, H)), weights(maps_ref[lanes + n].T))
            pushes = pushes + jnp.where(lane_line == s * chunks + h * blocks + step // LEN, pushed[0:1], 0.0)
    push_ref[...] = pushes

    def spread(table, columns, k, s):
        lane = s * chunks + k
        return jnp.sum(table[lane, :H, :] * columns[s], axis=0, keepdims=True)

    def starts(k, carry):
        for s in range(2):
            lane = s * chunks + k
            start_ref[pl.ds(lane, 1), :] = spread(prefix, columns_d, k, s) + prefix[lane, H:H + 1, :]
        return carry

    lax.fori_loop(0, chunks, starts, 0)

    def forward(j, carry):
        state, back0, back1 = carry
        rows = pl.ds(j, lanes, stride=LEN)
        k = chunks - 1 - j
        out = []
        for s, t in enumerate((back0, back1)):
            lane = s * chunks + k
            carry_ref[pl.ds(lane, 1), :] = t[0:1]
            out.append(t + times(t, turned[lane]) + push_ref[pl.ds(lane, 1), :])
        state = state + gain_ref[rows, :] * times(state, packed) + resid_ref[rows, :]
        traj_ref[rows, :] = state + guess_ref[rows, :]
        return state, out[0], out[1]

    nothing = jnp.zeros((16, H), F32)
    lax.fori_loop(0, LEN, forward, (start_ref[...], nothing, nothing))
    traj_copy = pltpu.make_async_copy(traj_ref, traj_hbm, load_sem.at[0])
    traj_copy.start()
    t_first = weights((pair[1, :H, :] - eye).T)
    t_after = weights((after - eye).T)
    t_rows = {k: weights((xbuf[k, :H, :] - eye).T) for k in range(1, nx - 1)}

    for copy in vz_copies:
        copy.wait_recv()
    total = jnp.zeros((H, H), F32)
    q_row = jnp.zeros((8, H), F32)
    for k in range(nz):
        if k > 0:
            total = total + jnp.where(k > z, ubuf[k] * qz[k, 0:1, :], 0.0)
        q_row = q_row + qz[k]
    qx[x] = q_row
    vx_copies = swap_copies(qx, "x", vxs, vxr, 8)
    for copy in vx_copies:
        copy.start()
    summed = lane_sum(total)
    near = summed[:, :H]
    for copy in vx_copies:
        copy.wait_recv()
    t = jnp.where(nx - 1 > x, jnp.broadcast_to(qx[nx - 1, 1:2, :], (16, H)), 0.0)
    for k in range(nx - 2, 0, -1):
        t = jnp.where(k > x, t + times(t, t_rows[k]) + qx[k, 1:2, :], t)
    lam_late = near + t + times(t, t_after)
    lam = lam_late + times(lam_late, t_first) + pull_late
    ends[1, c] = jnp.where(c == 0, lam[:8], lam_late[:8])
    tiles[1] = jnp.where(c == 0, lam_late[:8], lam[:8])
    lam_copy = remote(tiles.at[1], ends.at[1, c], core_send.at[3], core_recv.at[3], sibling)
    lam_copy.start()
    packed_t = weights(rate_t.T)
    lam_copy.wait_recv()
    columns_l = [jnp.broadcast_to(ends[1, s, 0:1, :], (H, H)).T for s in range(2)]

    def carries(k, carry):
        for s in range(2):
            lane = pl.ds(s * chunks + k, 1)
            carry_ref[lane, :] = carry_ref[lane, :] + spread(suffix, columns_l, k, s)
        return carry

    lax.fori_loop(0, chunks, carries, 0)

    def backward(j, adjoint):
        rows = pl.ds(LEN - 1 - j, lanes, stride=LEN)
        adjoint = adjoint + source_ref[rows, :]
        scaled = gain_ref[rows, :] * adjoint
        pre_ref[rows, :] = scaled
        return adjoint + times(scaled, packed_t)

    lax.fori_loop(0, LEN, backward, carry_ref[...])
    left_high, left_low = split(jnp.concatenate([prev_rows([edge[s, 7:8, :] * at_start for s in range(2)]), x_ref[...]], axis=1))
    right = wide(pre_ref[...])
    dims = (((0,), (0,)), ((), ()))
    both = lax.dot_general(left_high, right, dims, preferred_element_type=F32)
    both = both + lax.dot_general(left_low, right, dims, preferred_element_type=F32)
    sums = both[:, :H] + both[:, H:]
    grads[0:H // 8] = (sums[:H].T - sums[:H]).reshape(H // 8, 8, H)
    grads[H // 8:] = sums[H:].reshape(2 * H // 8, 8, H)

    share = grads.shape[0] // plane
    done = []
    for i in range(plane - 1):
        done.append(remote(
            grads.at[pl.ds(planes[i] * share, share)], parts.at[p], send1.at[i], recv1.at[i], plane_ids[i]
        ))
        done[-1].start()
    parts[p] = grads[pl.ds(p * share, share)]
    for copy in done:
        copy.wait_recv()
    shares[q] = jnp.sum(parts[...], axis=0)
    exchange = [
        remote(shares.at[q], shares.at[q], send2.at[i], recv2.at[i], column_ids[i]) for i in range(column - 1)
    ]
    for copy in exchange:
        copy.start()
    for copy in exchange:
        copy.wait_recv()
    mine = pl.ds(p * share, share)
    whole[mine] = jnp.sum(shares[...], axis=0)
    last = [
        remote(whole.at[mine], whole.at[mine], send3.at[i], recv3.at[i], plane_ids[i]) for i in range(plane - 1)
    ]
    for copy in last:
        copy.start()

    @pl.when(inner)
    def _():
        for copy in x_copies(x, True):
            copy.wait_send()

    @pl.when(jnp.logical_not(inner))
    def _():
        for copy in x_copies(x, False):
            copy.wait_send()

    traj_copy.wait()
    early = edge_copies + [core_copy, hit_copy, delta_copy, lam_copy] + z_copies + vz_copies + vx_copies
    for copy in early + done + exchange:
        copy.wait_send()
    for copy in last:
        copy.wait_recv()
    recur_ref[...] = whole[0:H // 8].reshape(H, H)
    gin_ref[...] = whole[H // 8:].reshape(2 * H, H)
    for copy in last:
        copy.wait_send()


def vmem(*dims):
    return pltpu.VMEM(dims, F32)


def out(*dims):
    return jax.ShapeDtypeStruct(dims, F32)


def on_device(inputs, guess_path, recur_weight, damping, in_weight, bias_term, targets, target_steps):
    seqs, steps, hidden = guess_path.shape
    features = inputs.shape[2]
    count = seqs * steps
    chunks = steps // LEN
    lanes = seqs * chunks
    nx, nz, nc, ny = (lax.axis_size(name) for name in ("x", "z", "core", "batch"))
    plane, column = nx * ny, nz * nc
    tiles = 3 * hidden // 8
    share = tiles // plane
    extra = count + 4 * LEN
    dma = pltpu.SemaphoreType.DMA
    traj, grad_recur, grad_in = pl.pallas_call(
        newton,
        out_shape=(out(count, hidden), out(hidden, hidden), out(features, hidden)),
        in_specs=[HBM] * 8,
        out_specs=[HBM, VM, VM],
        scratch_shapes=[
            vmem(count, features), vmem(count, hidden), vmem(hidden, hidden), vmem(1, hidden),
            vmem(features, hidden), vmem(1, hidden), vmem(4, hidden), pltpu.SMEM((seqs, 2), jnp.int32), dma((8,)),
            vmem(seqs, 8, hidden), vmem(extra, hidden), vmem(extra, hidden), vmem(lanes + 16, hidden),
            vmem(lanes + 4, hidden, hidden), vmem(chunks // 2, AUG, hidden), vmem(seqs, AUG, hidden),
            vmem(lanes, AUG, hidden), vmem(lanes, hidden, hidden), pltpu.VMEM((lanes, 2 * hidden, 2 * hidden), BF16),
            vmem(2, AUG, hidden), vmem(4, AUG, hidden), vmem(2, 2, AUG, hidden), vmem(nz, AUG, hidden),
            vmem(nz, hidden, hidden), vmem(nx, AUG, hidden), vmem(nz, 8, hidden), vmem(nx, 8, hidden),
            vmem(2, 8, hidden), vmem(2, seqs, 8, hidden),
            vmem(lanes, hidden), vmem(lanes, hidden), vmem(lanes, hidden), vmem(count, hidden), vmem(count, hidden),
            vmem(count, hidden),
            vmem(tiles, 8, hidden), vmem(plane, share, 8, hidden), vmem(column, share, 8, hidden), vmem(tiles, 8, hidden),
            dma((2,)), dma((2,)), dma((4,)), dma((4,)), dma((nz - 1,)), dma((nz - 1,)), dma((nx - 1,)), dma((nx - 1,)),
            dma((nz - 1,)), dma((nz - 1,)), dma((nx - 1,)), dma((nx - 1,)),
            dma((plane - 1,)), dma((plane - 1,)), dma((column - 1,)), dma((column - 1,)), dma((plane - 1,)),
            dma((plane - 1,)),
        ],
        compiler_params=pltpu.CompilerParams(
            collective_id=0, has_side_effects=True, vmem_limit_bytes=63 * 1024 * 1024
        ),
        name="newton",
    )(
        inputs.reshape(count, features), guess_path.reshape(count, hidden), recur_weight, damping.reshape(1, hidden),
        in_weight, bias_term.reshape(1, hidden), targets.reshape(-1, hidden), target_steps,
    )
    return traj.reshape(guess_path.shape), grad_recur, grad_in


def solution(mesh):
    torus = Mesh(mesh.devices.reshape(4, 8, 2, mesh.shape["batch"]), (*SEQ, "batch"))
    return jax.shard_map(
        on_device,
        mesh=torus,
        in_specs=(
            P("batch", SEQ, None), P("batch", SEQ, None), P(), P(), P(), P(), P("batch", SEQ, None), P("batch", SEQ),
        ),
        out_specs=(P("batch", SEQ, None), P(), P()),
        check_vma=False,
    )
```

time: 483 us -> 78 us (0.16)
  matrix products: 164 us -> 0 us
  blocking collectives: 100 us -> 0 us
  Pallas kernels: 0 us -> 73.9 us
  local copies, waits for them, and re-layouts: 75.6 us -> 3.29 us
  waiting for transfers between devices: 53.9 us -> 0 us
  starting transfers between devices: 37.8 us -> 0 us
  other arithmetic: 27.4 us -> 0 us
  between operations: 14.9 us -> 0.65 us
    dot_general x222 -> x0, matrix products: 164 us -> none  [the longest x16 61.8 us: compose(): jnp.dot(skew, maps.reshape(hidden, lane_count * hidden), precision=highest)]
    all_gather x10 -> x0, blocking collectives: 83.1 us -> none  [prefix_by_axis(): pieces = jax.tree.map(lambda part: lax.all_gather(part, axis), subtotal)]
    pallas_call x0 -> x1, Pallas kernels: none -> 73.9 us  [on_device(): pl.pallas_call(newton, out_shape=(out(count, hidden), out(hidden, hidden)...]
    all_to_all x7 -> x0, waiting for transfers between devices: 45.1 us -> none  [the longest x4 24.9 us: copy_for_each(): lax.all_to_all(jnp.broadcast_to(shard[None], (length, *shard.shape)), axi...]
    all_to_all x7 -> x0, starting transfers between devices: 32.9 us -> none  [the longest x4 18.5 us: copy_for_each(): lax.all_to_all(jnp.broadcast_to(shard[None], (length, *shard.shape)), axi...]
    while x97 -> x0, local copies, waits for them, and re-layouts: 31 us -> none
    squeeze x32 -> x0, local copies, waits for them, and re-layouts: 29.7 us -> none  [on_device(): lax.scan(chain, (unit_stack, seq_zero), (blocks, offsets))]
    add x89 -> x0, other arithmetic: 21 us -> none  [the longest x48 11.4 us: apply_map(): jnp.einsum('isj,sj->si', block_map, carry, precision=lax.Precision.HIGHEST)]
  transfers between devices with their start and end apart: 10 -> 0, of which waited for: 8 -> 0; matrix products, arithmetic and copies ran while one was open for 20% -> 0% of each run, Pallas kernels for 0% -> 0%
where the time goes in v2:
time: 78 us; the launch traced here: 77.8 us
  Pallas kernels  73.9 us (95%)
  local copies, waits for them, and re-layouts  3.29 us (4%)
    pallas_call x1, Pallas kernels, on_device(): pl.pallas_call(newton, out_shape=(out(count, hidden), out(hidden, hidden)...  73.9 us
    unnamed x7, local copies, waits for them, and re-layouts  3.29 us

profile of v2, /device:TPU:1, one launch (start us, length us, event | category | flops | bytes accessed | tf_op | source)
XLA Modules:
  0.0 77.8 jit_solution(5538251165395343172)
XLA Ops:
  0.6 73.9 %newton.1 = (f32[512,128]{1,0:T(8,128)}, f32[128,128]{1,0:T(8,128)}, f32[256,128]{1,0:T(8,128)}) custom-call(f32[512,256]{1,0:T(8,128)} %bitcast.6, f32[512,128]{1,0:T(8,128)} %bitcast.8, f32[128,128]{1,0:T(8,128)} %w_hbm.1, f32[1,128]{1,0:T(1,128)} %bitcast.10, f32[256,128]{1,0:T(8,128)} %u_hbm.1, f32[1,128]{1,0:T(1,128)} %bitcast.11, f32[4,128]{1,0:T(4,128)} %bitcast.9, ...), custom_call_target="tpu_custom_call" | custom-call | tf_op jit(solution)/shard_map/newton/pallas_call | solution.py:608
  74.5 0.0 copy-start.1
  74.5 1.7 %copy.14 = f32[2,256,128]{2,1,0:T(8,128)} copy(f32[2,256,128]{2,1,0:T(8,128)} %bitcast.7) | data formatting | bytes 524288
  76.2 0.0 copy-done.1
  76.2 0.0 copy-start
  76.2 0.6 copy.15
  76.9 0.3 copy-done
  77.2 0.7 copy.16
Async XLA Ops:
  74.5 1.7 %copy-start.1 = (f32[128,128]{1,0:T(8,128)S(1)}, f32[128,128]{1,0:T(8,128)}, u32[]{:S(2)}) copy-start(f32[128,128]{1,0:T(8,128)} %get-tuple-element.13) | copy-start | bytes 196612
  76.2 0.9 %copy-start = (f32[256,128]{1,0:T(8,128)S(1)}, f32[256,128]{1,0:T(8,128)}, u32[]{:S(2)}) copy-start(f32[256,128]{1,0:T(8,128)} %get-tuple-element.14) | copy-start | bytes 393220

commit v3 on v2

--- a/solution.py
+++ b/solution.py
@@ -11,6 +11,7 @@
 TBLK = 128
 AUG = 144
 SENT = 136
+DEPTH = 5
 SEQ = ("x", "z", "core")
 EULER = 0.02
 F32 = jnp.float32
@@ -73,8 +74,9 @@
     n = lax.axis_size(axis)
     me = lax.axis_index(axis)
     part = buf.at[me, pl.ds(0, rows)]
+    farthest_first = sorted(range(1, n), key=lambda d: -min(d, n - d))
     return [
-        remote(part, part, sends.at[d - 1], recvs.at[d - 1], {axis: lax.rem(me + d, n)}) for d in range(1, n)
+        remote(part, part, sends.at[d - 1], recvs.at[d - 1], {axis: lax.rem(me + d, n)}) for d in farthest_first
     ]
 
 
@@ -88,10 +90,10 @@
     traj_hbm, recur_ref, gin_ref,
     x_ref, guess_ref, w_ref, damp_ref, u_ref, bias_ref, target_ref, steps_ref, load_sem,
     edge, gain_ref, resid_ref, offs_ref, maps_ref, tree, totals, prefix, suffix, turned,
-    pair, hit_ref, hits, zbuf, ubuf, xbuf, qz, qx, tiles, ends,
+    pair, hit_ref, hits, zbuf, ubuf, xbuf, pulls, tiles, ends,
     start_ref, carry_ref, push_ref, source_ref, pre_ref, traj_ref,
     grads, parts, shares, whole,
-    edge_send, edge_recv, core_send, core_recv, zs, zr, xs, xr, vzs, vzr, vxs, vxr,
+    edge_send, edge_recv, core_send, core_recv, zs, zr, xs, xr, pull_send, pull_recv,
     send1, recv1, send2, recv2, send3, recv3,
 ):
     x, y, z, c = (lax.axis_index(name) for name in ("x", "batch", "z", "core"))
@@ -129,7 +131,16 @@
     following = along(lax.rem(place + 1, nx * column))
     preceding = along(lax.rem(place + nx * column - 1, nx * column))
     barrier = pltpu.get_barrier_semaphore()
-    greeted = plane_ids + column_ids + [following, preceding]
+    chips = nx * nz
+    chip = x * nz + z
+    chip_ids = []
+    for d in range(1, chips):
+        mate = lax.rem(chip + d, chips)
+        chip_ids.append({"x": mate // nz, "z": lax.rem(mate, nz)})
+    across = [
+        {"x": lax.rem(x + dx, nx), "z": lax.rem(z + dz, nz)} for dx in range(1, nx) for dz in range(1, nz)
+    ]
+    greeted = plane_ids + column_ids + across + [following, preceding]
     for target in greeted:
         pl.semaphore_signal(barrier, inc=1, device_id=target, device_id_type=MESH)
 
@@ -159,14 +170,10 @@
     resid_ref[0:count, :] = prev + EULER * activation - guess
     early_preact = [preact[s * steps:s * steps + 1] for s in range(2)]
 
-    pl.semaphore_wait(barrier, len(greeted))
     edge_copies = [
         remote(guess_ref.at[pl.ds((s + 1) * steps - 8, 8)], edge.at[s], edge_send.at[s], edge_recv.at[s], following)
         for s in range(2)
     ]
-    for copy in edge_copies:
-        copy.start()
-
     chunk_line = lax.broadcasted_iota(jnp.int32, (LEN, H), 0)
 
     def begin(s):
@@ -191,8 +198,8 @@
 
     def compose(s, begin_at, end_at):
         def body(i, carry):
-            for u in range(3):
-                j = 1 + 3 * i + u
+            for u in range(DEPTH):
+                j = 1 + DEPTH * i + u
                 rows = pl.ds(s * steps + j, chunks, stride=LEN)
                 step_maps(s * chunks, chunks, gain_ref[rows, :], resid_ref[rows, :])
             return carry
@@ -243,8 +250,12 @@
             copy.start()
 
     begin(0)
+    compose(0, 0, 1)
+    pl.semaphore_wait(barrier, len(greeted))
+    for copy in edge_copies:
+        copy.start()
+    compose(0, 1, (LEN - 1) // DEPTH)
     begin(1)
-    compose(0, 0, (LEN - 1) // 3)
     for copy in edge_copies:
         copy.wait_recv()
     at_start = jnp.where(place > 0, 1.0, 0.0)
@@ -261,13 +272,13 @@
     def _():
         core_copy.start()
 
-    compose(1, 0, 2)
+    compose(1, 0, 1)
 
     @pl.when(c == 0)
     def _():
         leave()
 
-    compose(1, 2, (LEN - 1) // 3)
+    compose(1, 1, (LEN - 1) // DEPTH)
     finish(1)
 
     @pl.when(c == 0)
@@ -298,8 +309,8 @@
 
     def compose_hits(begin_at, end_at):
         def body(i, carry):
-            for u in range(3):
-                j = 1 + 3 * i + u
+            for u in range(DEPTH):
+                j = 1 + DEPTH * i + u
                 step_maps(lanes, 4, hit_rows(gain_ref, j), hit_rows(resid_ref, j))
             return carry
 
@@ -311,7 +322,7 @@
     def _():
         leave()
 
-    compose_hits(2, (LEN - 1) // 3)
+    compose_hits(2, (LEN - 1) // DEPTH)
 
     start = jnp.concatenate([eye, jnp.zeros((16, H), F32)], axis=0)
 
@@ -424,9 +435,11 @@
         pull = pull + times(misses[i], t_hits[i])
     far = times(pull, t_ahead)
     line = lax.broadcasted_iota(jnp.int32, (8, H), 0)
-    qz[z] = jnp.where(line == 0, pull[0:1], far[0:1])
-    vz_copies = swap_copies(qz, "z", vzs, vzr, 8)
-    for copy in vz_copies:
+    pulls[chip] = jnp.where(line == 0, pull[0:1], far[0:1])
+    pull_copies = [
+        remote(pulls.at[chip], pulls.at[chip], pull_send.at[i], pull_recv.at[i], chip_ids[i]) for i in range(chips - 1)
+    ]
+    for copy in pull_copies:
         copy.start()
     v_late = v + times(v, w_first) + tail_of(pair[0, H:SENT, :])
     ends[0, c] = jnp.where(c == 0, v[:8], v_late[:8])
@@ -454,54 +467,36 @@
         lane = s * chunks + k
         return jnp.sum(table[lane, :H, :] * columns[s], axis=0, keepdims=True)
 
-    def starts(k, carry):
-        for s in range(2):
-            lane = s * chunks + k
-            start_ref[pl.ds(lane, 1), :] = spread(prefix, columns_d, k, s) + prefix[lane, H:H + 1, :]
-        return carry
-
-    lax.fori_loop(0, chunks, starts, 0)
-
-    def forward(j, carry):
-        state, back0, back1 = carry
-        rows = pl.ds(j, lanes, stride=LEN)
+    def local_back(j, carry):
         k = chunks - 1 - j
         out = []
-        for s, t in enumerate((back0, back1)):
+        for s, t in enumerate(carry):
             lane = s * chunks + k
             carry_ref[pl.ds(lane, 1), :] = t[0:1]
             out.append(t + times(t, turned[lane]) + push_ref[pl.ds(lane, 1), :])
-        state = state + gain_ref[rows, :] * times(state, packed) + resid_ref[rows, :]
-        traj_ref[rows, :] = state + guess_ref[rows, :]
-        return state, out[0], out[1]
+        return tuple(out)
 
     nothing = jnp.zeros((16, H), F32)
-    lax.fori_loop(0, LEN, forward, (start_ref[...], nothing, nothing))
-    traj_copy = pltpu.make_async_copy(traj_ref, traj_hbm, load_sem.at[0])
-    traj_copy.start()
+    lax.fori_loop(0, chunks, local_back, (nothing, nothing), unroll=True)
     t_first = weights((pair[1, :H, :] - eye).T)
     t_after = weights((after - eye).T)
     t_rows = {k: weights((xbuf[k, :H, :] - eye).T) for k in range(1, nx - 1)}
 
-    for copy in vz_copies:
+    for copy in pull_copies:
         copy.wait_recv()
     total = jnp.zeros((H, H), F32)
-    q_row = jnp.zeros((8, H), F32)
-    for k in range(nz):
-        if k > 0:
-            total = total + jnp.where(k > z, ubuf[k] * qz[k, 0:1, :], 0.0)
-        q_row = q_row + qz[k]
-    qx[x] = q_row
-    vx_copies = swap_copies(qx, "x", vxs, vxr, 8)
-    for copy in vx_copies:
-        copy.start()
-    summed = lane_sum(total)
-    near = summed[:, :H]
-    for copy in vx_copies:
-        copy.wait_recv()
-    t = jnp.where(nx - 1 > x, jnp.broadcast_to(qx[nx - 1, 1:2, :], (16, H)), 0.0)
+    for k in range(1, nz):
+        total = total + jnp.where(k > z, ubuf[k] * pulls[x * nz + k, 0:1, :], 0.0)
+    near = lane_sum(total)
+    row_pulls = []
+    for k in range(nx):
+        row = pulls[k * nz]
+        for i in range(1, nz):
+            row = row + pulls[k * nz + i]
+        row_pulls.append(row)
+    t = jnp.where(nx - 1 > x, jnp.broadcast_to(row_pulls[nx - 1][1:2], (16, H)), 0.0)
     for k in range(nx - 2, 0, -1):
-        t = jnp.where(k > x, t + times(t, t_rows[k]) + qx[k, 1:2, :], t)
+        t = jnp.where(k > x, t + times(t, t_rows[k]) + row_pulls[k][1:2], t)
     lam_late = near + t + times(t, t_after)
     lam = lam_late + times(lam_late, t_first) + pull_late
     ends[1, c] = jnp.where(c == 0, lam[:8], lam_late[:8])
@@ -527,7 +522,7 @@
         pre_ref[rows, :] = scaled
         return adjoint + times(scaled, packed_t)
 
-    lax.fori_loop(0, LEN, backward, carry_ref[...])
+    lax.fori_loop(0, LEN, backward, carry_ref[...], unroll=True)
     left_high, left_low = split(jnp.concatenate([prev_rows([edge[s, 7:8, :] * at_start for s in range(2)]), x_ref[...]], axis=1))
     right = wide(pre_ref[...])
     dims = (((0,), (0,)), ((), ()))
@@ -545,6 +540,23 @@
         ))
         done[-1].start()
     parts[p] = grads[pl.ds(p * share, share)]
+
+    def starts(k, carry):
+        for s in range(2):
+            lane = s * chunks + k
+            start_ref[pl.ds(lane, 1), :] = spread(prefix, columns_d, k, s) + prefix[lane, H:H + 1, :]
+        return carry
+
+    def forward(j, state):
+        rows = pl.ds(j, lanes, stride=LEN)
+        state = state + gain_ref[rows, :] * times(state, packed) + resid_ref[rows, :]
+        traj_ref[rows, :] = state + guess_ref[rows, :]
+        return state
+
+    lax.fori_loop(0, chunks, starts, 0)
+    lax.fori_loop(0, LEN, forward, start_ref[...], unroll=True)
+    traj_copy = pltpu.make_async_copy(traj_ref, traj_hbm, load_sem.at[0])
+    traj_copy.start()
     for copy in done:
         copy.wait_recv()
     shares[q] = jnp.sum(parts[...], axis=0)
@@ -574,7 +586,7 @@
             copy.wait_send()
 
     traj_copy.wait()
-    early = edge_copies + [core_copy, hit_copy, delta_copy, lam_copy] + z_copies + vz_copies + vx_copies
+    early = edge_copies + [core_copy, hit_copy, delta_copy, lam_copy] + z_copies + pull_copies
     for copy in early + done + exchange:
         copy.wait_send()
     for copy in last:
@@ -617,13 +629,13 @@
             vmem(lanes + 4, hidden, hidden), vmem(chunks // 2, AUG, hidden), vmem(seqs, AUG, hidden),
             vmem(lanes, AUG, hidden), vmem(lanes, hidden, hidden), pltpu.VMEM((lanes, 2 * hidden, 2 * hidden), BF16),
             vmem(2, AUG, hidden), vmem(4, AUG, hidden), vmem(2, 2, AUG, hidden), vmem(nz, AUG, hidden),
-            vmem(nz, hidden, hidden), vmem(nx, AUG, hidden), vmem(nz, 8, hidden), vmem(nx, 8, hidden),
+            vmem(nz, hidden, hidden), vmem(nx, AUG, hidden), vmem(nx * nz, 8, hidden),
             vmem(2, 8, hidden), vmem(2, seqs, 8, hidden),
             vmem(lanes, hidden), vmem(lanes, hidden), vmem(lanes, hidden), vmem(count, hidden), vmem(count, hidden),
             vmem(count, hidden),
             vmem(tiles, 8, hidden), vmem(plane, share, 8, hidden), vmem(column, share, 8, hidden), vmem(tiles, 8, hidden),
             dma((2,)), dma((2,)), dma((4,)), dma((4,)), dma((nz - 1,)), dma((nz - 1,)), dma((nx - 1,)), dma((nx - 1,)),
-            dma((nz - 1,)), dma((nz - 1,)), dma((nx - 1,)), dma((nx - 1,)),
+            dma((nx * nz - 1,)), dma((nx * nz - 1,)),
             dma((plane - 1,)), dma((plane - 1,)), dma((column - 1,)), dma((column - 1,)), dma((plane - 1,)),
             dma((plane - 1,)),
         ],

time: 78 us -> 75.3 us (0.965)
  Pallas kernels: 73.9 us -> 71.2 us
    pallas_call x1, Pallas kernels: 73.9 us -> 71.2 us  [on_device(): pl.pallas_call(newton, out_shape=(out(count, hidden), out(hidden, hidden)...]
where the time goes in v3:
time: 75.3 us; the launch traced here: 75.1 us
  Pallas kernels  71.2 us (95%)
  local copies, waits for them, and re-layouts  3.29 us (4%)
    pallas_call x1, Pallas kernels, on_device(): pl.pallas_call(newton, out_shape=(out(count, hidden), out(hidden, hidden)...  71.2 us
    unnamed x7, local copies, waits for them, and re-layouts  3.29 us

profile of v3, /device:TPU:1, one launch (start us, length us, event | category | flops | bytes accessed | tf_op | source)
XLA Modules:
  0.0 75.1 jit_solution(5643088688193833760)
XLA Ops:
  0.6 71.2 %newton.1 = (f32[512,128]{1,0:T(8,128)}, f32[128,128]{1,0:T(8,128)}, f32[256,128]{1,0:T(8,128)}) custom-call(f32[512,256]{1,0:T(8,128)} %bitcast.6, f32[512,128]{1,0:T(8,128)} %bitcast.8, f32[128,128]{1,0:T(8,128)} %w_hbm.1, f32[1,128]{1,0:T(1,128)} %bitcast.10, f32[256,128]{1,0:T(8,128)} %u_hbm.1, f32[1,128]{1,0:T(1,128)} %bitcast.11, f32[4,128]{1,0:T(4,128)} %bitcast.9, ...), custom_call_target="tpu_custom_call" | custom-call | tf_op jit(solution)/shard_map/newton/pallas_call | solution.py:620
  71.8 0.0 copy-start.1
  71.9 1.7 %copy.14 = f32[2,256,128]{2,1,0:T(8,128)} copy(f32[2,256,128]{2,1,0:T(8,128)} %bitcast.7) | data formatting | bytes 524288
  73.6 0.0 copy-done.1
  73.6 0.0 copy-start
  73.6 0.6 copy.15
  74.2 0.3 copy-done
  74.5 0.7 copy.16
Async XLA Ops:
  71.8 1.7 %copy-start.1 = (f32[128,128]{1,0:T(8,128)S(1)}, f32[128,128]{1,0:T(8,128)}, u32[]{:S(2)}) copy-start(f32[128,128]{1,0:T(8,128)} %get-tuple-element.13) | copy-start | bytes 196612
  73.6 0.9 %copy-start = (f32[256,128]{1,0:T(8,128)S(1)}, f32[256,128]{1,0:T(8,128)}, u32[]{:S(2)}) copy-start(f32[256,128]{1,0:T(8,128)} %get-tuple-element.14) | copy-start | bytes 393220

commit v4 on v3

--- a/solution.py
+++ b/solution.py
@@ -18,7 +18,7 @@
 BF16 = jnp.bfloat16
 MESH = pl.DeviceIdType.MESH
 VM = pl.BlockSpec(memory_space=pltpu.VMEM)
-HBM = pl.BlockSpec(memory_space=pl.ANY)
+HBM = pl.BlockSpec(memory_space=pltpu.HBM)
 
 
 def split(value):
@@ -87,12 +87,12 @@
 
 def newton(
     x_hbm, guess_hbm, w_hbm, damp_hbm, u_hbm, bias_hbm, target_hbm, steps_hbm,
-    traj_hbm, recur_ref, gin_ref,
+    traj_ref, whole,
     x_ref, guess_ref, w_ref, damp_ref, u_ref, bias_ref, target_ref, steps_ref, load_sem,
     edge, gain_ref, resid_ref, offs_ref, maps_ref, tree, totals, prefix, suffix, turned,
     pair, hit_ref, hits, zbuf, ubuf, xbuf, pulls, tiles, ends,
-    start_ref, carry_ref, push_ref, source_ref, pre_ref, traj_ref,
-    grads, parts, shares, whole,
+    start_ref, carry_ref, push_ref, source_ref, pre_ref,
+    grads, parts, shares,
     edge_send, edge_recv, core_send, core_recv, zs, zr, xs, xr, pull_send, pull_recv,
     send1, recv1, send2, recv2, send3, recv3,
 ):
@@ -137,12 +137,8 @@
     for d in range(1, chips):
         mate = lax.rem(chip + d, chips)
         chip_ids.append({"x": mate // nz, "z": lax.rem(mate, nz)})
-    across = [
-        {"x": lax.rem(x + dx, nx), "z": lax.rem(z + dz, nz)} for dx in range(1, nx) for dz in range(1, nz)
-    ]
-    greeted = plane_ids + column_ids + across + [following, preceding]
-    for target in greeted:
-        pl.semaphore_signal(barrier, inc=1, device_id=target, device_id_type=MESH)
+    z_ids = [{"z": lax.rem(z + d, nz)} for d in range(1, nz)]
+    greeted = plane_ids + z_ids + [sibling, following, preceding]
 
     eye = unit()
     loads[0].wait()
@@ -151,6 +147,8 @@
     packed = weights(rate_t)
     for load in loads[2:]:
         load.wait()
+    for target in greeted:
+        pl.semaphore_signal(barrier, inc=1, device_id=target, device_id_type=MESH)
     guess = guess_ref[...]
 
     def prev_rows(firsts):
@@ -250,11 +248,11 @@
             copy.start()
 
     begin(0)
-    compose(0, 0, 1)
+    compose(0, 0, 2)
     pl.semaphore_wait(barrier, len(greeted))
     for copy in edge_copies:
         copy.start()
-    compose(0, 1, (LEN - 1) // DEPTH)
+    compose(0, 2, (LEN - 1) // DEPTH)
     begin(1)
     for copy in edge_copies:
         copy.wait_recv()
@@ -435,7 +433,7 @@
         pull = pull + times(misses[i], t_hits[i])
     far = times(pull, t_ahead)
     line = lax.broadcasted_iota(jnp.int32, (8, H), 0)
-    pulls[chip] = jnp.where(line == 0, pull[0:1], far[0:1])
+    pulls[chip] = jnp.concatenate([pull[0:1], far[0:1]], axis=0)
     pull_copies = [
         remote(pulls.at[chip], pulls.at[chip], pull_send.at[i], pull_recv.at[i], chip_ids[i]) for i in range(chips - 1)
     ]
@@ -555,8 +553,6 @@
 
     lax.fori_loop(0, chunks, starts, 0)
     lax.fori_loop(0, LEN, forward, start_ref[...], unroll=True)
-    traj_copy = pltpu.make_async_copy(traj_ref, traj_hbm, load_sem.at[0])
-    traj_copy.start()
     for copy in done:
         copy.wait_recv()
     shares[q] = jnp.sum(parts[...], axis=0)
@@ -585,16 +581,28 @@
         for copy in x_copies(x, False):
             copy.wait_send()
 
-    traj_copy.wait()
     early = edge_copies + [core_copy, hit_copy, delta_copy, lam_copy] + z_copies + pull_copies
     for copy in early + done + exchange:
         copy.wait_send()
     for copy in last:
         copy.wait_recv()
-    recur_ref[...] = whole[0:H // 8].reshape(H, H)
-    gin_ref[...] = whole[H // 8:].reshape(2 * H, H)
     for copy in last:
         copy.wait_send()
+
+
+def deliver(traj_ref, whole_ref, traj_hbm, recur_hbm, gin_hbm, sems):
+    rows = recur_hbm.shape[0]
+    copies = [
+        pltpu.make_async_copy(src, dst, sems.at[i])
+        for i, (src, dst) in enumerate((
+            (traj_ref, traj_hbm), (whole_ref.at[pl.ds(0, rows)], recur_hbm),
+            (whole_ref.at[pl.ds(rows, gin_hbm.shape[0])], gin_hbm),
+        ))
+    ]
+    for copy in copies:
+        copy.start()
+    for copy in copies:
+        copy.wait()
 
 
 def vmem(*dims):
@@ -617,11 +625,11 @@
     share = tiles // plane
     extra = count + 4 * LEN
     dma = pltpu.SemaphoreType.DMA
-    traj, grad_recur, grad_in = pl.pallas_call(
+    traj, whole = pl.pallas_call(
         newton,
-        out_shape=(out(count, hidden), out(hidden, hidden), out(features, hidden)),
+        out_shape=(out(count, hidden), out(tiles, 8, hidden)),
         in_specs=[HBM] * 8,
-        out_specs=[HBM, VM, VM],
+        out_specs=[VM, VM],
         scratch_shapes=[
             vmem(count, features), vmem(count, hidden), vmem(hidden, hidden), vmem(1, hidden),
             vmem(features, hidden), vmem(1, hidden), vmem(4, hidden), pltpu.SMEM((seqs, 2), jnp.int32), dma((8,)),
@@ -629,24 +637,35 @@
             vmem(lanes + 4, hidden, hidden), vmem(chunks // 2, AUG, hidden), vmem(seqs, AUG, hidden),
             vmem(lanes, AUG, hidden), vmem(lanes, hidden, hidden), pltpu.VMEM((lanes, 2 * hidden, 2 * hidden), BF16),
             vmem(2, AUG, hidden), vmem(4, AUG, hidden), vmem(2, 2, AUG, hidden), vmem(nz, AUG, hidden),
-            vmem(nz, hidden, hidden), vmem(nx, AUG, hidden), vmem(nx * nz, 8, hidden),
+            vmem(nz, hidden, hidden), vmem(nx, AUG, hidden), vmem(nx * nz, 2, hidden),
             vmem(2, 8, hidden), vmem(2, seqs, 8, hidden),
             vmem(lanes, hidden), vmem(lanes, hidden), vmem(lanes, hidden), vmem(count, hidden), vmem(count, hidden),
-            vmem(count, hidden),
-            vmem(tiles, 8, hidden), vmem(plane, share, 8, hidden), vmem(column, share, 8, hidden), vmem(tiles, 8, hidden),
+            vmem(tiles, 8, hidden), vmem(plane, share, 8, hidden), vmem(column, share, 8, hidden),
             dma((2,)), dma((2,)), dma((4,)), dma((4,)), dma((nz - 1,)), dma((nz - 1,)), dma((nx - 1,)), dma((nx - 1,)),
             dma((nx * nz - 1,)), dma((nx * nz - 1,)),
             dma((plane - 1,)), dma((plane - 1,)), dma((column - 1,)), dma((column - 1,)), dma((plane - 1,)),
             dma((plane - 1,)),
         ],
         compiler_params=pltpu.CompilerParams(
-            collective_id=0, has_side_effects=True, vmem_limit_bytes=63 * 1024 * 1024
+            collective_id=0, has_side_effects=True, vmem_limit_bytes=40 * 1024 * 1024
         ),
         name="newton",
     )(
-        inputs.reshape(count, features), guess_path.reshape(count, hidden), recur_weight, damping.reshape(1, hidden),
-        in_weight, bias_term.reshape(1, hidden), targets.reshape(-1, hidden), target_steps,
+        *(pltpu.with_memory_space_constraint(value, pltpu.HBM) for value in (
+            inputs.reshape(count, features), guess_path.reshape(count, hidden), recur_weight, damping.reshape(1, hidden),
+            in_weight, bias_term.reshape(1, hidden), targets.reshape(-1, hidden), target_steps,
+        ))
     )
+    any_space = pl.BlockSpec(memory_space=pl.ANY)
+    traj, grad_recur, grad_in = pl.pallas_call(
+        deliver,
+        out_shape=(out(count, hidden), out(hidden, hidden), out(features, hidden)),
+        in_specs=[VM, VM],
+        out_specs=[any_space] * 3,
+        scratch_shapes=[dma((3,))],
+        compiler_params=pltpu.CompilerParams(vmem_limit_bytes=4 * 1024 * 1024),
+        name="deliver",
+    )(traj, whole.reshape(3 * hidden, hidden))
     return traj.reshape(guess_path.shape), grad_recur, grad_in
 
 

time: 75.3 us -> 70.3 us (0.934)
  local copies, waits for them, and re-layouts: 3.29 us -> 0 us
  Pallas kernels: 71.2 us -> 69.4 us
    unnamed x7 -> x0, local copies, waits for them, and re-layouts: 3.29 us -> none
    pallas_call x1 -> x2, Pallas kernels: 71.2 us -> 69.4 us  [the longest x1 68.6 us: on_device(): pl.pallas_call(newton, out_shape=(out(count, hidden), out(tiles, 8, hidde...]
where the time goes in v4:
time: 70.3 us; the launch traced here: 70.2 us
  Pallas kernels  69.4 us (99%)
  between operations  0.8 us (1%)
    pallas_call x1, Pallas kernels, on_device(): pl.pallas_call(newton, out_shape=(out(count, hidden), out(tiles, 8, hidde...  68.6 us

profile of v4, /device:TPU:1, one launch (start us, length us, event | category | flops | bytes accessed | tf_op | source)
XLA Modules:
  0.0 70.2 jit_solution(14536797807309268823)
XLA Ops:
  0.6 68.6 %newton.1 = (f32[512,128]{1,0:T(8,128)S(1)}, f32[48,8,128]{2,1,0:T(8,128)S(1)}) custom-call(f32[512,256]{1,0:T(8,128)} %bitcast.8, f32[512,128]{1,0:T(8,128)} %bitcast.9, f32[128,128]{1,0:T(8,128)} %w_hbm.1, f32[1,128]{1,0:T(1,128)} %bitcast.11, f32[256,128]{1,0:T(8,128)} %u_hbm.1, f32[1,128]{1,0:T(1,128)} %bitcast.12, f32[4,128]{1,0:T(4,128)} %bitcast.10, ...), custom_call_target="tpu_custom_call" | custom-call | tf_op jit(solution)/shard_map/newton/pallas_call | solution.py:628
  69.3 0.8 %deliver.1 = (f32[512,128]{1,0:T(8,128)}, f32[128,128]{1,0:T(8,128)}, f32[256,128]{1,0:T(8,128)}) custom-call(f32[512,128]{1,0:T(8,128)S(1)} %get-tuple-element.8.traj_ref, f32[384,128]{1,0:T(8,128)S(1)} %bitcast.7), custom_call_target="tpu_custom_call" | custom-call | tf_op jit(solution)/shard_map/deliver/pallas_call | solution.py:660

commit v5 on v4

--- a/solution.py
+++ b/solution.py
@@ -76,7 +76,7 @@
     part = buf.at[me, pl.ds(0, rows)]
     farthest_first = sorted(range(1, n), key=lambda d: -min(d, n - d))
     return [
-        remote(part, part, sends.at[d - 1], recvs.at[d - 1], {axis: lax.rem(me + d, n)}) for d in farthest_first
+        (d, remote(part, part, sends.at[d - 1], recvs.at[d - 1], {axis: lax.rem(me + d, n)})) for d in farthest_first
     ]
 
 
@@ -93,7 +93,7 @@
     pair, hit_ref, hits, zbuf, ubuf, xbuf, pulls, tiles, ends,
     start_ref, carry_ref, push_ref, source_ref, pre_ref,
     grads, parts, shares,
-    edge_send, edge_recv, core_send, core_recv, zs, zr, xs, xr, pull_send, pull_recv,
+    edge_send, edge_recv, core_send, core_recv, zs, zr, relay_send, relay_recv, xs, xr, pull_send, pull_recv,
     send1, recv1, send2, recv2, send3, recv3,
 ):
     x, y, z, c = (lax.axis_index(name) for name in ("x", "batch", "z", "core"))
@@ -235,7 +235,20 @@
     core_copy = remote(
         totals.at[other, pl.ds(0, SENT)], pair.at[c, pl.ds(0, SENT)], core_send.at[0], core_recv.at[0], sibling
     )
-    z_copies = swap_copies(zbuf, "z", zs, zr, SENT)
+    quarter = nz // 4
+    pieces = (pl.ds(0, 72), pl.ds(72, SENT - 72))
+    relays = []
+    for i, (toward, piece) in enumerate(zip((quarter, nz - quarter), pieces)):
+        part = zbuf.at[lax.rem(z + nz - toward, nz), piece]
+        relays.append(remote(part, part, relay_send.at[i], relay_recv.at[i], {"z": lax.rem(z + toward, nz)}))
+    first_legs = [copy for d, copy in swap_copies(zbuf, "z", zs, zr, SENT) if d in (quarter, nz - quarter)]
+    other_legs = [copy for d, copy in swap_copies(zbuf, "z", zs, zr, SENT) if d not in (quarter, nz // 2, nz - quarter)]
+
+    def pass_on():
+        for copy in first_legs:
+            copy.wait_recv()
+        for copy in relays:
+            copy.start()
 
     def leave():
         core_copy.wait_recv()
@@ -244,7 +257,7 @@
             jnp.concatenate([pair[0, :H, :], tail_of(pair[0, H:SENT, :])], axis=0),
             pair[1, :H, :], tail_of(pair[1, H:SENT, :]), eye,
         )
-        for copy in z_copies:
+        for copy in first_legs + other_legs:
             copy.start()
 
     begin(0)
@@ -282,6 +295,7 @@
     @pl.when(c == 0)
     def _():
         core_copy.start()
+        pass_on()
 
     for s in range(2):
         for h in range(2):
@@ -333,6 +347,11 @@
         return tuple(out)
 
     lax.fori_loop(0, chunks, chain, (start, start))
+
+    @pl.when(c == 1)
+    def _():
+        pass_on()
+
     block_line = lax.broadcasted_iota(jnp.int32, (TBLK, H), 0)
     map_line = jnp.zeros((AUG, H), jnp.int32)
     for s in range(2):
@@ -366,8 +385,39 @@
 
     lax.fori_loop(0, chunks, back_chain, (eye, eye))
 
-    for copy in z_copies:
+    for copy in other_legs + relays:
         copy.wait_recv()
+    size = nz
+    while size > 1:
+        for k in range(size // 2):
+            table = zbuf if size == nz else tree
+            ends_at = [tail_of(table[2 * k + i, H:SENT, :]) for i in range(2)]
+            left = jnp.concatenate([table[2 * k, :H, :], ends_at[0]], axis=0)
+            joined = then(left, table[2 * k + 1, :H, :], ends_at[1], eye)
+            if size == 2:
+                xbuf[x] = joined
+            else:
+                tree[k] = joined
+        size //= 2
+    inner = jnp.logical_and(x > 0, x < nx - 1)
+
+    def x_copy(slot, full, d):
+        part = xbuf.at[slot, pl.ds(0, SENT) if full else pl.ds(H, 8)]
+        return remote(part, part, xs.at[d - 1], xr.at[d - 1], {"x": lax.rem(x + d, nx)})
+
+    def x_copies(slot, full):
+        return [x_copy(slot, full, d) for d in range(1, nx)]
+
+    @pl.when(inner)
+    def _():
+        for copy in x_copies(x, True):
+            copy.start()
+
+    @pl.when(jnp.logical_not(inner))
+    def _():
+        for copy in x_copies(x, False):
+            copy.start()
+
     run = jnp.concatenate([zbuf[0, :H, :], tail_of(zbuf[0, H:SENT, :])], axis=0)
     ahead = start
     after = eye
@@ -378,26 +428,6 @@
         offset = tail_of(zbuf[k, H:SENT, :])
         run = run + moved[:AUG] + jnp.concatenate([jnp.zeros((H, H), F32), offset], axis=0)
         after = jnp.where(k > z, after + moved[AUG:], after)
-    xbuf[x] = run
-    inner = jnp.logical_and(x > 0, x < nx - 1)
-
-    def x_copy(slot, full, d):
-        part = xbuf.at[slot, pl.ds(0, SENT) if full else pl.ds(H, 8)]
-        return remote(part, part, xs.at[d - 1], xr.at[d - 1], {"x": lax.rem(x + d, nx)})
-
-    def x_copies(slot, full):
-        return [x_copy(slot, full, d) for d in range(1, nx)]
-
-    @pl.when(inner)
-    def _():
-        for copy in x_copies(x, True):
-            copy.start()
-
-    @pl.when(jnp.logical_not(inner))
-    def _():
-        for copy in x_copies(x, False):
-            copy.start()
-
     hit_copy.wait_recv()
     first_map = jnp.concatenate([pair[0, :H, :], tail_of(pair[0, H:SENT, :])], axis=0)
     late = [then(first_map, hits[1, h, :H, :], hits[1, h, H:, :], eye) for h in range(2)]
@@ -502,17 +532,23 @@
     lam_copy = remote(tiles.at[1], ends.at[1, c], core_send.at[3], core_recv.at[3], sibling)
     lam_copy.start()
     packed_t = weights(rate_t.T)
+
+    def add_carries(s):
+        spread_row = jnp.broadcast_to(ends[1, s, 0:1, :], (H, H)).T
+
+        def body(i, carry):
+            for u in range(4):
+                lane = s * chunks + 4 * i + u
+                rows = pl.ds(lane, 1)
+                moved = jnp.sum(suffix[lane] * spread_row, axis=0, keepdims=True)
+                carry_ref[rows, :] = carry_ref[rows, :] + moved
+            return carry
+
+        lax.fori_loop(0, chunks // 4, body, 0)
+
+    add_carries(c)
     lam_copy.wait_recv()
-    columns_l = [jnp.broadcast_to(ends[1, s, 0:1, :], (H, H)).T for s in range(2)]
-
-    def carries(k, carry):
-        for s in range(2):
-            lane = pl.ds(s * chunks + k, 1)
-            carry_ref[lane, :] = carry_ref[lane, :] + spread(suffix, columns_l, k, s)
-        return carry
-
-    lax.fori_loop(0, chunks, carries, 0)
-
+    add_carries(other)
     def backward(j, adjoint):
         rows = pl.ds(LEN - 1 - j, lanes, stride=LEN)
         adjoint = adjoint + source_ref[rows, :]
@@ -581,7 +617,7 @@
         for copy in x_copies(x, False):
             copy.wait_send()
 
-    early = edge_copies + [core_copy, hit_copy, delta_copy, lam_copy] + z_copies + pull_copies
+    early = edge_copies + [core_copy, hit_copy, delta_copy, lam_copy] + first_legs + other_legs + relays + pull_copies
     for copy in early + done + exchange:
         copy.wait_send()
     for copy in last:
@@ -641,7 +677,7 @@
             vmem(2, 8, hidden), vmem(2, seqs, 8, hidden),
             vmem(lanes, hidden), vmem(lanes, hidden), vmem(lanes, hidden), vmem(count, hidden), vmem(count, hidden),
             vmem(tiles, 8, hidden), vmem(plane, share, 8, hidden), vmem(column, share, 8, hidden),
-            dma((2,)), dma((2,)), dma((4,)), dma((4,)), dma((nz - 1,)), dma((nz - 1,)), dma((nx - 1,)), dma((nx - 1,)),
+            dma((2,)), dma((2,)), dma((4,)), dma((4,)), dma((nz - 1,)), dma((nz - 1,)), dma((2,)), dma((2,)), dma((nx - 1,)), dma((nx - 1,)),
             dma((nx * nz - 1,)), dma((nx * nz - 1,)),
             dma((plane - 1,)), dma((plane - 1,)), dma((column - 1,)), dma((column - 1,)), dma((plane - 1,)),
             dma((plane - 1,)),

time: 70.3 us -> 70.5 us (level)
  no operation moved by 1% of the time
where the time goes in v5:
time: 70.5 us; the launch traced here: 70.4 us
  Pallas kernels  69.6 us (99%)
  between operations  0.8 us (1%)
    pallas_call x1, Pallas kernels, on_device(): pl.pallas_call(newton, out_shape=(out(count, hidden), out(tiles, 8, hidde...  68.8 us

profile of v5, /device:TPU:1, one launch (start us, length us, event | category | flops | bytes accessed | tf_op | source)
XLA Modules:
  0.0 70.4 jit_solution(16571789072222110091)
XLA Ops:
  0.6 68.8 %newton.1 = (f32[512,128]{1,0:T(8,128)S(1)}, f32[48,8,128]{2,1,0:T(8,128)S(1)}) custom-call(f32[512,256]{1,0:T(8,128)} %bitcast.8, f32[512,128]{1,0:T(8,128)} %bitcast.9, f32[128,128]{1,0:T(8,128)} %w_hbm.1, f32[1,128]{1,0:T(1,128)} %bitcast.11, f32[256,128]{1,0:T(8,128)} %u_hbm.1, f32[1,128]{1,0:T(1,128)} %bitcast.12, f32[4,128]{1,0:T(4,128)} %bitcast.10, ...), custom_call_target="tpu_custom_call" | custom-call | tf_op jit(solution)/shard_map/newton/pallas_call | solution.py:664
  69.4 0.8 %deliver.1 = (f32[512,128]{1,0:T(8,128)}, f32[128,128]{1,0:T(8,128)}, f32[256,128]{1,0:T(8,128)}) custom-call(f32[512,128]{1,0:T(8,128)S(1)} %get-tuple-element.8.traj_ref, f32[384,128]{1,0:T(8,128)S(1)} %bitcast.7), custom_call_target="tpu_custom_call" | custom-call | tf_op jit(solution)/shard_map/deliver/pallas_call | solution.py:696

commit v6 on v5

--- a/solution.py
+++ b/solution.py
@@ -119,10 +119,15 @@
     plane, column = nx * ny, nz * nc
     p = x * ny + y
     q = z * nc + c
-    planes = [lax.rem(p + d, plane) for d in range(1, plane)]
-    columns = [lax.rem(q + d, column) for d in range(1, column)]
-    plane_ids = [{"x": mate // ny, "batch": lax.rem(mate, ny)} for mate in planes]
-    column_ids = [{"z": mate // nc, "core": lax.rem(mate, nc)} for mate in columns]
+
+    def mates(axes):
+        (one, here, first), (two, there, second) = axes
+        offsets = [(i, j) for i in range(first) for j in range(second) if i or j]
+        offsets.sort(key=lambda o: -min(o[0], first - o[0]) - (0 if two == "core" else min(o[1], second - o[1])))
+        return [{one: lax.rem(here + i, first), two: lax.rem(there + j, second)} for i, j in offsets]
+
+    plane_ids = mates((("x", x, nx), ("batch", y, ny)))
+    planes = [mate["x"] * ny + mate["batch"] for mate in plane_ids]
     place = x * column + q
 
     def along(where):
@@ -133,10 +138,6 @@
     barrier = pltpu.get_barrier_semaphore()
     chips = nx * nz
     chip = x * nz + z
-    chip_ids = []
-    for d in range(1, chips):
-        mate = lax.rem(chip + d, chips)
-        chip_ids.append({"x": mate // nz, "z": lax.rem(mate, nz)})
     z_ids = [{"z": lax.rem(z + d, nz)} for d in range(1, nz)]
     greeted = plane_ids + z_ids + [sibling, following, preceding]
 
@@ -328,13 +329,13 @@
 
         lax.fori_loop(begin_at, end_at, body, 0)
 
-    compose_hits(0, 2)
+    compose_hits(0, 1)
 
     @pl.when(c == 1)
     def _():
         leave()
 
-    compose_hits(2, (LEN - 1) // DEPTH)
+    compose_hits(1, (LEN - 1) // DEPTH)
 
     start = jnp.concatenate([eye, jnp.zeros((16, H), F32)], axis=0)
 
@@ -383,7 +384,7 @@
             out.append(carry[s] + times(carry[s], turn))
         return tuple(out)
 
-    lax.fori_loop(0, chunks, back_chain, (eye, eye))
+    halfway = lax.fori_loop(0, chunks // 2, back_chain, (eye, eye))
 
     for copy in other_legs + relays:
         copy.wait_recv()
@@ -439,6 +440,7 @@
     t_ahead = weights(ahead[:H].T)
     miss_rows = [hits[0, h, H:, :] for h in range(2)] + [late[h][H:] for h in range(2)]
 
+    lax.fori_loop(chunks // 2, chunks, back_chain, halfway)
     for d in range(1, nx):
         source = lax.rem(x + nx - d, nx)
         source_inner = jnp.logical_and(source > 0, source < nx - 1)
@@ -464,6 +466,7 @@
     far = times(pull, t_ahead)
     line = lax.broadcasted_iota(jnp.int32, (8, H), 0)
     pulls[chip] = jnp.concatenate([pull[0:1], far[0:1]], axis=0)
+    chip_ids = mates((("x", x, nx), ("z", z, nz)))
     pull_copies = [
         remote(pulls.at[chip], pulls.at[chip], pull_send.at[i], pull_recv.at[i], chip_ids[i]) for i in range(chips - 1)
     ]
@@ -592,6 +595,7 @@
     for copy in done:
         copy.wait_recv()
     shares[q] = jnp.sum(parts[...], axis=0)
+    column_ids = mates((("z", z, nz), ("core", c, nc)))
     exchange = [
         remote(shares.at[q], shares.at[q], send2.at[i], recv2.at[i], column_ids[i]) for i in range(column - 1)
     ]

time: 70.5 us -> 67.3 us (0.955)
  Pallas kernels: 69.6 us -> 66.4 us
    pallas_call x1, Pallas kernels: 68.8 us -> 65.6 us  [on_device(): pl.pallas_call(newton, out_shape=(out(count, hidden), out(tiles, 8, hidde...]
where the time goes in v6:
time: 67.3 us; the launch traced here: 67.2 us
  Pallas kernels  66.4 us (99%)
  between operations  0.8 us (1%)
    pallas_call x1, Pallas kernels, on_device(): pl.pallas_call(newton, out_shape=(out(count, hidden), out(tiles, 8, hidde...  65.6 us

profile of v6, /device:TPU:1, one launch (start us, length us, event | category | flops | bytes accessed | tf_op | source)
XLA Modules:
  0.0 67.2 jit_solution(6210910740131152842)
XLA Ops:
  0.6 65.6 %newton.1 = (f32[512,128]{1,0:T(8,128)S(1)}, f32[48,8,128]{2,1,0:T(8,128)S(1)}) custom-call(f32[512,256]{1,0:T(8,128)} %bitcast.8, f32[512,128]{1,0:T(8,128)} %bitcast.9, f32[128,128]{1,0:T(8,128)} %w_hbm.1, f32[1,128]{1,0:T(1,128)} %bitcast.11, f32[256,128]{1,0:T(8,128)} %u_hbm.1, f32[1,128]{1,0:T(1,128)} %bitcast.12, f32[4,128]{1,0:T(4,128)} %bitcast.10, ...), custom_call_target="tpu_custom_call" | custom-call | tf_op jit(solution)/shard_map/newton/pallas_call | solution.py:668
  66.3 0.8 %deliver.1 = (f32[512,128]{1,0:T(8,128)}, f32[128,128]{1,0:T(8,128)}, f32[256,128]{1,0:T(8,128)}) custom-call(f32[512,128]{1,0:T(8,128)S(1)} %get-tuple-element.8.traj_ref, f32[384,128]{1,0:T(8,128)S(1)} %bitcast.7), custom_call_target="tpu_custom_call" | custom-call | tf_op jit(solution)/shard_map/deliver/pallas_call | solution.py:700

commit v7 on v6

--- a/solution.py
+++ b/solution.py
@@ -347,11 +347,13 @@
             out.append(then(carry[s], maps_ref[lane], offset_of(lane), eye))
         return tuple(out)
 
-    lax.fori_loop(0, chunks, chain, (start, start))
+    middle = lax.fori_loop(0, chunks // 2, chain, (start, start))
 
     @pl.when(c == 1)
     def _():
         pass_on()
+
+    lax.fori_loop(chunks // 2, chunks, chain, middle)
 
     block_line = lax.broadcasted_iota(jnp.int32, (TBLK, H), 0)
     map_line = jnp.zeros((AUG, H), jnp.int32)
@@ -384,7 +386,7 @@
             out.append(carry[s] + times(carry[s], turn))
         return tuple(out)
 
-    halfway = lax.fori_loop(0, chunks // 2, back_chain, (eye, eye))
+    partway = lax.fori_loop(0, 3 * chunks // 8, back_chain, (eye, eye))
 
     for copy in other_legs + relays:
         copy.wait_recv()
@@ -440,7 +442,7 @@
     t_ahead = weights(ahead[:H].T)
     miss_rows = [hits[0, h, H:, :] for h in range(2)] + [late[h][H:] for h in range(2)]
 
-    lax.fori_loop(chunks // 2, chunks, back_chain, halfway)
+    lax.fori_loop(3 * chunks // 8, chunks, back_chain, partway)
     for d in range(1, nx):
         source = lax.rem(x + nx - d, nx)
         source_inner = jnp.logical_and(source > 0, source < nx - 1)

time: 67.3 us -> 67.2 us (level)
  no operation moved by 1% of the time
where the time goes in v7:
time: 67.2 us; the launch traced here: 67.1 us
  Pallas kernels  66.3 us (99%)
  between operations  0.8 us (1%)
    pallas_call x1, Pallas kernels, on_device(): pl.pallas_call(newton, out_shape=(out(count, hidden), out(tiles, 8, hidde...  65.5 us

profile of v7, /device:TPU:1, one launch (start us, length us, event | category | flops | bytes accessed | tf_op | source)
XLA Modules:
  0.0 67.1 jit_solution(7039513243401649954)
XLA Ops:
  0.6 65.5 %newton.1 = (f32[512,128]{1,0:T(8,128)S(1)}, f32[48,8,128]{2,1,0:T(8,128)S(1)}) custom-call(f32[512,256]{1,0:T(8,128)} %bitcast.8, f32[512,128]{1,0:T(8,128)} %bitcast.9, f32[128,128]{1,0:T(8,128)} %w_hbm.1, f32[1,128]{1,0:T(1,128)} %bitcast.11, f32[256,128]{1,0:T(8,128)} %u_hbm.1, f32[1,128]{1,0:T(1,128)} %bitcast.12, f32[4,128]{1,0:T(4,128)} %bitcast.10, ...), custom_call_target="tpu_custom_call" | custom-call | tf_op jit(solution)/shard_map/newton/pallas_call | solution.py:670
  66.1 0.8 %deliver.1 = (f32[512,128]{1,0:T(8,128)}, f32[128,128]{1,0:T(8,128)}, f32[256,128]{1,0:T(8,128)}) custom-call(f32[512,128]{1,0:T(8,128)S(1)} %get-tuple-element.8.traj_ref, f32[384,128]{1,0:T(8,128)S(1)} %bitcast.7), custom_call_target="tpu_custom_call" | custom-call | tf_op jit(solution)/shard_map/deliver/pallas_call | solution.py:702
